TPU v7x, 256 devices: a whole 4x4x8 slice. The times are simulated.
256 devices in a mesh: req: 32 (over z, y), tp: 8 (over x, core).
Axes of the slice: x: 4, y: 4, z: 8, core: 2. Of those that a mesh axis runs over, the one named last changes fastest.
Arguments:
- hidden: bfloat16 [9472, 5120], P('req', 'tp'), may hold values from -6 to 6
- raw_q: bfloat16 [9472, 3072], P('req', 'tp'), may hold values from -70 to 70
- raw_k: bfloat16 [9472, 3072], P('req', 'tp'), may hold values from -70 to 70
- raw_v: bfloat16 [9472, 3072], P('req', 'tp'), may hold values from -6 to 6
- q_gain: float32 [3072], P('tp'), may hold values from 0.5 to 2
- k_gain: float32 [3072], P('tp'), may hold values from 0.5 to 2
- out_weight: bfloat16 [3072, 5120], P('tp'), may hold values from -0.109375 to 0.109375
- post_gain: float32 [5120], P('tp'), may hold values from 0.25 to 1.75
- prefix_keys: bfloat16 [32, 32, 128, 3072], P(None, 'req', None, 'tp'), may hold values from -420 to 420
- prefix_values: bfloat16 [32, 32, 128, 3072], P(None, 'req', None, 'tp'), may hold values from -6 to 6
- key_cache: bfloat16 [256, 128, 3072], P('req', None, 'tp'), may hold values from -420 to 420
- value_cache: bfloat16 [256, 128, 3072], P('req', None, 'tp'), may hold values from -6 to 6
- slot_owner: int32 [256], P('req'), may hold values from -1 to 255, as said below
- slot_page: int32 [256], P('req'), may hold values from 0 to 127, as said below
- cache_lengths: int32 [256], replicated, may hold values from 0 to 16384, as said below
- span_offsets: int32 [32], replicated, may hold values from 0 to 4096
Outputs:
- new_hidden: bfloat16 [9472, 5120], P('req', 'tp')
Inputs may be any that keep to these rules, and one draw needn't show every extreme that they name: Each pool slot holds one page of decode request slot_owner[s], or nothing where it is -1. No page of a request is held twice, and a request holding c pages holds pages 0 to c - 1. `slot_page`: 0 for a slot that holds nothing. `cache_lengths`: A request holding c pages of the pool has a length from (c - 1) * 128 + 1 to c * 128, and 0 where c = 0.
All inputs are finite; a program needn't handle non-finite values.
Results may differ from a plain program's by a relative error of at most 0.0076.
Values may be sent and summed in bfloat16 or wider, within the bound.
A program may use at most 128 MiB of HBM per device.

v0:
```python
import jax
import jax.numpy as jnp
from jax import lax
from jax.sharding import PartitionSpec as P

HD = 128
SPAN = 288
DEC = 8


EPSILON = 1e-06
THETA = 500000.0
NEGATIVE = -1e30


def rotate(values, positions):
    half_width = values.shape[-1] // 2
    frequency = THETA ** (-(jnp.arange(half_width, dtype=jnp.float32) * 2.0 / values.shape[-1]))
    angles = positions.astype(jnp.float32)[:, None] * frequency[None, :]
    cosine = jnp.cos(angles)[:, None, :]
    sine_part = jnp.sin(angles)[:, None, :]
    first_half = values[..., :half_width]
    second = values[..., half_width:]
    return jnp.concatenate(
        [first_half * cosine - second * sine_part, second * cosine + first_half * sine_part], -1
    )


def softmax_part(scores, key_mask, values, form):
    masked = jnp.where(key_mask, scores, NEGATIVE)
    top_score = jnp.max(masked, -1)
    exp_terms = jnp.where(key_mask, jnp.exp(masked - top_score[..., None]), 0.0)
    weight_sum = jnp.sum(exp_terms, -1)
    numerator = jnp.einsum(
        form, exp_terms.astype(jnp.bfloat16), values, preferred_element_type=jnp.float32
    )
    return (top_score, weight_sum, numerator)


def merge_parts(top_scores, weight_sums, numerators):
    best_score = jnp.max(top_scores, 0)
    factor = jnp.exp(top_scores - best_score[None])
    weight_sum = jnp.sum(factor * weight_sums, 0)
    numerator = jnp.sum(factor[..., None] * numerators, 0)
    return numerator / weight_sum[..., None]


def body(
    hidden,
    raw_q,
    raw_k,
    raw_v,
    q_gain,
    k_gain,
    out_weight,
    post_gain,
    prefix_keys,
    prefix_values,
    key_cache,
    value_cache,
    slot_owner,
    slot_page,
    cache_lengths,
    span_offsets,
):
    groups = lax.axis_size("req")
    my_group = lax.axis_index("req")
    tp_count = lax.axis_size("tp")
    tp_index = lax.axis_index("tp")
    rows_group = SPAN + DEC
    local_width = raw_q.shape[1]
    local_heads = local_width // HD
    requests = groups * DEC
    score_scale = HD ** (-0.5)
    page_rows = key_cache.shape[1]
    own_lengths = lax.dynamic_slice_in_dim(cache_lengths, my_group * DEC, DEC)
    positions = jnp.concatenate(
        [span_offsets[my_group] + jnp.arange(SPAN, dtype=jnp.int32), own_lengths]
    )
    float_query = raw_q.astype(jnp.float32)
    float_key = raw_k.astype(jnp.float32)
    query_power, key_power = lax.psum(
        (jnp.sum(float_query * float_query, 1), jnp.sum(float_key * float_key, 1)), "tp"
    )
    full_width = local_width * tp_count
    normed_query = (
        float_query * lax.rsqrt(query_power / full_width + EPSILON)[:, None] * q_gain[None, :]
    )
    normed_key = float_key * lax.rsqrt(key_power / full_width + EPSILON)[:, None] * k_gain[None, :]
    query = rotate(normed_query.reshape(rows_group, local_heads, HD), positions).astype(
        jnp.bfloat16
    )
    key_rows = rotate(normed_key.reshape(rows_group, local_heads, HD), positions).astype(
        jnp.bfloat16
    )
    value_rows = raw_v.reshape(rows_group, local_heads, HD)
    causal = jnp.arange(SPAN)[:, None] >= jnp.arange(SPAN)[None, :]
    self_scores = (
        jnp.einsum(
            "qhd,khd->qhk", query[:SPAN], key_rows[:SPAN], preferred_element_type=jnp.float32
        )
        * score_scale
    )
    self_top, self_total, self_numerator = softmax_part(
        self_scores, causal[:, None, :], value_rows[:SPAN], "qhk,khd->qhd"
    )
    own_scores = (
        jnp.sum(query[SPAN:].astype(jnp.float32) * key_rows[SPAN:].astype(jnp.float32), -1)
        * score_scale
    )
    own_total = jnp.ones_like(own_scores)
    own_numerator = value_rows[SPAN:].astype(jnp.float32)
    everyone = lax.all_gather(query, "req", axis=0, tiled=True)
    everyone = everyone.reshape(groups, rows_group, local_heads, HD)
    pages_here = prefix_keys.shape[1]
    block_keys = prefix_keys.reshape(groups, pages_here * page_rows, local_heads, HD)
    block_values = prefix_values.reshape(groups, pages_here * page_rows, local_heads, HD)
    key_pos = my_group * pages_here * page_rows + jnp.arange(
        pages_here * page_rows, dtype=jnp.int32
    )
    key_mask = key_pos[None, :] < span_offsets[:, None]
    scores = (
        jnp.einsum(
            "gqhd,gkhd->gqhk", everyone[:, :SPAN], block_keys, preferred_element_type=jnp.float32
        )
        * score_scale
    )
    pre_top, pre_total, pre_numerator = softmax_part(
        scores, key_mask[:, None, None, :], block_values, "gqhk,gkhd->gqhd"
    )
    live_slot = slot_owner >= 0
    owner_index = jnp.maximum(slot_owner, 0)
    slot_queries = everyone[:, SPAN:].reshape(requests, local_heads, HD)[owner_index]
    slot_keys = key_cache.reshape(key_cache.shape[0], page_rows, local_heads, HD)
    slot_values = value_cache.reshape(value_cache.shape[0], page_rows, local_heads, HD)
    scores = (
        jnp.einsum("shd,sphd->shp", slot_queries, slot_keys, preferred_element_type=jnp.float32)
        * score_scale
    )
    key_pos = slot_page[:, None] * page_rows + jnp.arange(page_rows, dtype=jnp.int32)[None, :]
    key_mask = live_slot[:, None] & (key_pos < cache_lengths[owner_index][:, None])
    top_score, weight_sum, numerator = softmax_part(
        scores, key_mask[:, None, :], slot_values, "shp,sphd->shd"
    )
    member = slot_owner[None, :] == jnp.arange(requests, dtype=jnp.int32)[:, None]
    best_score = jnp.max(jnp.where(member[:, :, None], top_score[None], NEGATIVE), 1)
    factor = jnp.where(member[:, :, None], jnp.exp(top_score[None] - best_score[:, None]), 0.0)
    request_total = jnp.einsum("rsh,sh->rh", factor, weight_sum, precision=lax.Precision.HIGHEST)
    request_numerator = jnp.einsum(
        "rsh,shd->rhd", factor, numerator, precision=lax.Precision.HIGHEST
    )
    send_top = jnp.concatenate([pre_top, best_score.reshape(groups, DEC, local_heads)], 1).reshape(
        groups * rows_group, local_heads
    )
    send_total = jnp.concatenate(
        [pre_total, request_total.reshape(groups, DEC, local_heads)], 1
    ).reshape(groups * rows_group, local_heads)
    send_numerator = jnp.concatenate(
        [pre_numerator, request_numerator.reshape(groups, DEC, local_heads, HD)], 1
    ).reshape(groups * rows_group, local_heads, HD)
    back_top, back_total, back_numerator = (
        lax.all_to_all(send_top, "req", split_axis=0, concat_axis=0, tiled=True),
        lax.all_to_all(send_total, "req", split_axis=0, concat_axis=0, tiled=True),
        lax.all_to_all(send_numerator, "req", split_axis=0, concat_axis=0, tiled=True),
    )
    local_top = jnp.concatenate([self_top, own_scores], 0)
    local_total = jnp.concatenate([self_total, own_total], 0)
    local_numerator = jnp.concatenate([self_numerator, own_numerator], 0)
    merged = merge_parts(
        jnp.concatenate([back_top.reshape(groups, rows_group, local_heads), local_top[None]], 0),
        jnp.concatenate(
            [back_total.reshape(groups, rows_group, local_heads), local_total[None]], 0
        ),
        jnp.concatenate(
            [back_numerator.reshape(groups, rows_group, local_heads, HD), local_numerator[None]], 0
        ),
    )
    attention = merged.reshape(rows_group, local_width).astype(jnp.bfloat16)
    share_width = post_gain.shape[0]
    projected = lax.psum(jnp.dot(attention, out_weight, preferred_element_type=jnp.float32), "tp")
    inverse = lax.rsqrt(jnp.mean(projected * projected, 1) + EPSILON)
    my_share = lax.dynamic_slice_in_dim(projected, tp_index * share_width, share_width, 1)
    normed = my_share * inverse[:, None]
    return (hidden.astype(jnp.float32) + normed * post_gain[None, :]).astype(jnp.bfloat16)


def solution(mesh):
    return jax.shard_map(
        body,
        mesh=mesh,
        in_specs=(
            P("req", "tp"),
            P("req", "tp"),
            P("req", "tp"),
            P("req", "tp"),
            P("tp"),
            P("tp"),
            P("tp", None),
            P("tp"),
            P(None, "req", None, "tp"),
            P(None, "req", None, "tp"),
            P("req", None, "tp"),
            P("req", None, "tp"),
            P("req"),
            P("req"),
            P(),
            P(),
        ),
        out_specs=P("req", "tp"),
        check_vma=False,
    )
```

profile of v0, /device:TPU:1, one launch (start us, length us, event | category | flops | bytes accessed | tf_op | source)
XLA Modules:
  0.0 842.2 jit_solution(3925593860115718974)
XLA Ops:
  6.6 1.2 dynamic_slice.9
  7.8 0.6 iota_add_fusion
  8.5 1.1 fusion.22
  9.5 1.1 fusion.24
  10.6 15.0 %all-reduce.1 = (f32[296]{0:T(512)S(1)}, f32[296]{0:T(512)S(1)}) all-reduce(f32[296]{0:T(512)S(1)} %fusion.24, f32[296]{0:T(512)S(1)} %fusion.22), channel_id=1, replica_groups=mesh['req'=32,'tp'=8] {'tp'}, use_global_device_ids=true, to_apply=%region_6.7 | all-reduce | flops 592 | bytes 4736 | tf_op jit(solution)/shard_map/psum | solution.py:82
  25.6 1.1 fusion.25
  26.9 1.0 fusion.23
  28.1 1.4 fusion.74
  29.5 1.5 fusion.75
  31.1 0.6 multiply_cosine_fusion
  31.7 2.8 subtract_convert_fusion.1
  34.6 0.7 copy-done.4
  35.3 0.8 pad_maximum_fusion.3
  36.2 0.6 gather_fusion
  36.8 2.3 copy.97
  39.2 2.3 copy.104
  41.5 2.9 copy.94
  44.4 3.5 copy.102
  48.1 81.2 %all-gather.2.cloned.1.call-done = bf16[9472,3,128]{2,0,1:T(8,128)(2,1)} async-done(((bf16[296,3,128]{2,0,1:T(8,128)(2,1)}), bf16[9472,3,128]{2,0,1:T(8,128)(2,1)}) %all-gather.2.cloned.1.call-update) | async-done | bytes 7274512 | tf_op jit(solution)/shard_map/all_gather | solution.py:113
  129.3 0.9 slice_bitcast_fusion.1
  130.5 0.6 gather_fusion.1
  131.0 1.4 fusion.47
  132.6 0.8 fusion.57
  133.6 1.6 fusion.45
  135.2 1.3 convolution_bitcast_fusion.2
  136.5 14.0 %bitcast_reduce_fusion = (f32[32,288,3]{1,2,0:T(4,128)S(1)}, f32[32,3,288,128]{3,2,1,0:T(8,128)}) fusion(pred[32,128]{1,0:T(8,128)(4,1)S(1)} %broadcast_compare_fusion, bf16[32,128,3,128]{1,3,2,0:T(8,128)(2,1)} %bitcast.96, bf16[32,296,3,128]{3,1,0,2:T(8,128)(2,1)} %bitcast.102), kind=kOutput, calls=%fused_computation.6 | convolution fusion | flops 916558848 | bytes 24494080 | tf_op jit(solution)/shard_map/gqhd,gkhd->gqhk/dot_general | solution.py:123
  150.5 0.8 pad_maximum_fusion.1
  151.3 5.8 all-to-all-start
  157.1 11.8 %fusion.3 = f32[32,288,3]{1,2,0:T(4,128)} fusion(f32[32,3,288,128]{3,2,1,0:T(8,128)} %get-tuple-element.28, f32[32,288,3]{1,2,0:T(4,128)S(1)} %get-tuple-element.27, pred[32,128]{1,0:T(8,128)(4,1)S(1)} %broadcast_compare_fusion), kind=kLoop, calls=%fused_computation.10 | loop fusion | flops 17667072 | bytes 14381056 | tf_op jit(solution)/shard_map/reduce_sum | solution.py:33
  168.9 10.0 %convolution_bitcast_fusion = f32[32,288,3,128]{3,1,2,0:T(8,128)} fusion(bf16[32,128,3,128]{1,3,2,0:T(8,128)(2,1)S(1)} %bitcast.95, f32[32,3,288,128]{3,2,1,0:T(8,128)S(1)} %copy-done.1, f32[32,288,3]{1,2,0:T(4,128)S(1)} %get-tuple-element.27, pred[32,128]{1,0:T(8,128)(4,1)S(1)} %broadcast_compare_fusion), kind=kOutput, calls=%fused_computation.12 | convolution fusion | flops 923664384 | bytes 31571968 | tf_op jit(solution)/shard_map/gqhk,gkhd->gqhd/dot_general | solution.py:34
  179.2 1.2 copy.105
  180.4 1.7 pad_maximum_fusion.2
  182.1 9.0 %all-to-all-start.2 = ((f32[32,296,3]{1,2,0:T(4,128)}), f32[32,296,3]{1,2,0:T(4,128)S(1)}, u32[]{:S(2)}, u32[]{:S(2)}) async-start(f32[32,296,3]{1,2,0:T(4,128)} %pad_maximum_fusion.2), calls=%async_computation.2 | async-start | bytes 393216 | tf_op jit(solution)/shard_map/all_to_all | solution.py:163
  191.2 11.1 %pad_maximum_fusion = f32[32,296,3,128]{3,1,2,0:T(8,128)} fusion(f32[32,288,3,128]{3,1,2,0:T(8,128)} %convolution_bitcast_fusion, f32[256,3,128]{2,0,1:T(8,128)S(1)} %copy.105), kind=kLoop, calls=%fused_computation.4 | loop fusion | flops 3637248 | bytes 29097984 | tf_op jit(solution)/shard_map/concatenate | solution.py:158
  202.3 11.1 %copy.107 = f32[32,296,3,128]{3,1,0,2:T(8,128)} copy(f32[32,296,3,128]{3,1,2,0:T(8,128)} %pad_maximum_fusion) | data formatting | bytes 29097984 | tf_op jit(solution)/shard_map/concatenate | solution.py:158
  213.4 35.5 %copy.108 = f32[9472,3,128]{2,1,0:T(4,128)} copy(f32[9472,3,128]{2,0,1:T(8,128)} %bitcast.94) | data formatting | bytes 29097984 | tf_op jit(solution)/shard_map/reshape | solution.py:160
  249.0 9.5 %all-to-all-start.1 = ((f32[9472,3,128]{2,1,0:T(4,128)}), f32[9472,3,128]{2,1,0:T(4,128)}, u32[]{:S(2)}, u32[]{:S(2)}) async-start(f32[9472,3,128]{2,1,0:T(4,128)} %copy.108), calls=%async_computation.1 | async-start | bytes 38797312 | tf_op jit(solution)/shard_map/all_to_all | solution.py:164
  258.4 0.3 all-reduce.4.cloned.1.call-start
  259.0 0.5 fusion.76
  259.4 0.3 fusion.16
  259.8 0.5 convolution_bitcast_fusion.1
  260.6 449.8 %all-to-all-done.1 = f32[9472,3,128]{2,1,0:T(4,128)} async-done(((f32[9472,3,128]{2,1,0:T(4,128)}), f32[9472,3,128]{2,1,0:T(4,128)}, u32[]{:S(2)}, u32[]{:S(2)}) %all-to-all-start.1) | async-done | bytes 14549024 | tf_op jit(solution)/shard_map/all_to_all | solution.py:164
  710.5 8.4 copy.111
  718.8 4.9 fusion
  723.8 4.4 fusion.26
  728.3 101.8 %all-reduce.4.cloned.1.call-done = f32[296,5120]{1,0:T(8,128)} async-done(((f32[296,5120]{1,0:T(8,128)}), f32[296,5120]{1,0:T(8,128)}) %all-reduce.4.cloned.1.call-update) | async-done | bytes 6062096 | tf_op jit(solution)/shard_map/psum | solution.py:180
  830.1 3.2 multiply_reduce_fusion
  833.3 2.1 add_convert_fusion
  (72 shorter events, 2.3 us)
Async XLA Ops:
  6.5 24.5 %copy-start = (s32[256]{0:T(256)S(1)}, s32[256]{0:T(256)}, u32[]{:S(2)}) copy-start(s32[256]{0:T(256)} %param.30) | copy-start | bytes 3076
  6.5 29.6 %copy-start.13 = (s32[8]{0:T(128)S(1)}, s32[8]{0:T(128)}, u32[]{:S(2)}) copy-start(s32[8]{0:T(128)} %param.28) | copy-start | bytes 100
  6.5 122.8 %all-gather.2.cloned.1.call-start = ((), (), s32[]{:S(2)}) async-start(), calls=%async_computation.3 | async-start | bytes 7501824 | tf_op jit(solution)/shard_map/all_gather | solution.py:113
  31.0 10.5 %copy-start.3 = (bf16[32,1,128,384]{3,2,1,0:T(8,128)(2,1)S(1)}, bf16[32,1,128,384]{3,2,1,0:T(8,128)(2,1)}, u32[]{:S(2)}) copy-start(bf16[32,1,128,384]{3,2,1,0:T(8,128)(2,1)} %param.24) | copy-start | bytes 9437188
  34.6 0.7 copy-start.4
  34.6 0.8 copy-start.6
  39.2 8.7 %copy-start.16 = (s32[8]{0:T(128)S(1)}, s32[8]{0:T(128)}, u32[]{:S(2)}) copy-start(s32[8]{0:T(128)} %param.29) | copy-start | bytes 100
  39.2 8.9 %copy-start.14 = (s32[32]{0:T(128)S(1)}, s32[32]{0:T(128)}, u32[]{:S(2)}) copy-start(s32[32]{0:T(128)} %param.31) | copy-start | bytes 388
  151.3 30.8 %all-to-all-start = ((f32[32,296,3]{1,2,0:T(4,128)}), f32[32,296,3]{1,2,0:T(4,128)S(1)}, u32[]{:S(2)}, u32[]{:S(2)}) async-start(f32[32,296,3]{1,2,0:T(4,128)} %pad_maximum_fusion.1), calls=%async_computation | async-start | bytes 393216 | tf_op jit(solution)/shard_map/all_to_all | solution.py:162
  157.0 11.8 %copy-start.1 = (f32[32,3,288,128]{3,2,1,0:T(8,128)S(1)}, f32[32,3,288,128]{3,2,1,0:T(8,128)}, u32[]{:S(2)}) copy-start(f32[32,3,288,128]{3,2,1,0:T(8,128)} %get-tuple-element.28) | copy-start | bytes 42467332
  168.9 10.0 %copy-start.12 = (f32[8,3]{0,1:T(4,128)S(1)}, f32[8,3]{0,1:T(4,128)}, u32[]{:S(2)}) copy-start(f32[8,3]{0,1:T(4,128)} %get-tuple-element.19) | copy-start | bytes 292
  182.1 66.9 %all-to-all-start.2 = ((f32[32,296,3]{1,2,0:T(4,128)}), f32[32,296,3]{1,2,0:T(4,128)S(1)}, u32[]{:S(2)}, u32[]{:S(2)}) async-start(f32[32,296,3]{1,2,0:T(4,128)} %pad_maximum_fusion.2), calls=%async_computation.2 | async-start | bytes 393216 | tf_op jit(solution)/shard_map/all_to_all | solution.py:163
  248.9 9.8 %copy-start.5 = (bf16[296,3,64]{2,0,1:T(8,128)(2,1)S(1)}, bf16[296,3,64]{2,0,1:T(8,128)(2,1)}, u32[]{:S(2)}) copy-start(bf16[296,3,64]{2,0,1:T(8,128)(2,1)} %copy-done.4) | copy-start | bytes 340996
  248.9 9.8 %copy-start.7 = (bf16[296,3,64]{2,0,1:T(8,128)(2,1)S(1)}, bf16[296,3,64]{2,0,1:T(8,128)(2,1)}, u32[]{:S(2)}) copy-start(bf16[296,3,64]{2,0,1:T(8,128)(2,1)} %copy-done.6) | copy-start | bytes 340996
  248.9 9.8 %copy-start.8 = (bf16[296,3,64]{2,0,1:T(8,128)(2,1)S(1)}, bf16[296,3,64]{2,0,1:T(8,128)(2,1)}, u32[]{:S(2)}) copy-start(bf16[296,3,64]{2,0,1:T(8,128)(2,1)} %get-tuple-element.17) | copy-start | bytes 340996
  248.9 9.8 %copy-start.9 = (bf16[296,3,64]{2,0,1:T(8,128)(2,1)S(1)}, bf16[296,3,64]{2,0,1:T(8,128)(2,1)}, u32[]{:S(2)}) copy-start(bf16[296,3,64]{2,0,1:T(8,128)(2,1)} %get-tuple-element.18) | copy-start | bytes 340996
  248.9 10.8 %copy-start.15 = (bf16[296,384]{1,0:T(8,128)(2,1)S(1)}, bf16[296,384]{1,0:T(8,128)(2,1)}, u32[]{:S(2)}) copy-start(bf16[296,384]{1,0:T(8,128)(2,1)} %param.19) | copy-start | bytes 681988
  249.0 461.5 %all-to-all-start.1 = ((f32[9472,3,128]{2,1,0:T(4,128)}), f32[9472,3,128]{2,1,0:T(4,128)}, u32[]{:S(2)}, u32[]{:S(2)}) async-start(f32[9472,3,128]{2,1,0:T(4,128)} %copy.108), calls=%async_computation.1 | async-start | bytes 38797312 | tf_op jit(solution)/shard_map/all_to_all | solution.py:164
  258.4 571.6 %all-reduce.4.cloned.1.call-start = ((), (), s32[]{:S(2)}) async-start(), calls=%async_computation.4 | async-start | bytes 12124160 | tf_op jit(solution)/shard_map/psum | solution.py:180
  718.8 5.0 copy-start.2
  728.2 105.0 %copy-start.10 = (bf16[296,640]{1,0:T(8,128)(2,1)S(1)}, bf16[296,640]{1,0:T(8,128)(2,1)}, u32[]{:S(2)}) copy-start(bf16[296,640]{1,0:T(8,128)(2,1)} %param.16) | copy-start | bytes 1136644
  728.2 105.0 %copy-start.11 = (f32[640]{0:T(1024)S(1)}, f32[640]{0:T(1024)}, u32[]{:S(2)}) copy-start(f32[640]{0:T(1024)} %param.23) | copy-start | bytes 7684
Sparse Core Ops, SparseCore 0:
  36.3 93.0 all-gather.1
  728.4 101.6 all-reduce.3
where the time goes:
time: 843 us; the launch traced here: 842 us
  waiting for transfers between devices  633 us (75%)
  local copies, waits for them, and re-layouts  75.1 us (9%)
  other arithmetic  46.9 us (6%)
  matrix products  34 us (4%)
  starting transfers between devices  24.5 us (3%)
  blocking collectives  15 us (2%)
  between operations  13.8 us (2%)
    all_to_all x1, waiting for transfers between devices, body(): lax.all_to_all(send_numerator, 'req', split_axis=0, concat_axis=0, tiled=...  450 us
    psum x1, waiting for transfers between devices, body(): lax.psum(jnp.dot(attention, out_weight, preferred_element_type=jnp.float3...  102 us
    all_gather x1, waiting for transfers between devices, body(): everyone = lax.all_gather(query, 'req', axis=0, tiled=True)  81.2 us
    reshape x1, local copies, waits for them, and re-layouts, body(): send_numerator = jnp.concatenate([pre_numerator, request_numerator.reshap...  35.5 us
  transfers between devices with their start and end apart: 5, of which 3 were waited for; matrix products, arithmetic and copies ran while one was open for 11% of the time, Pallas kernels for 0%

commit v1 on v0

--- a/solution.py
+++ b/solution.py
@@ -66,13 +66,19 @@
     groups = lax.axis_size("req")
     my_group = lax.axis_index("req")
     tp_count = lax.axis_size("tp")
-    tp_index = lax.axis_index("tp")
     rows_group = SPAN + DEC
     local_width = raw_q.shape[1]
     local_heads = local_width // HD
     requests = groups * DEC
     score_scale = HD ** (-0.5)
     page_rows = key_cache.shape[1]
+
+    own_keys = lax.all_to_all(prefix_keys, "req", split_axis=0, concat_axis=1, tiled=True)
+    own_values = lax.all_to_all(prefix_values, "req", split_axis=0, concat_axis=1, tiled=True)
+    prefix_len = own_keys.shape[1] * page_rows
+    own_keys = own_keys.reshape(prefix_len, local_heads, HD)
+    own_values = own_values.reshape(prefix_len, local_heads, HD)
+
     own_lengths = lax.dynamic_slice_in_dim(cache_lengths, my_group * DEC, DEC)
     positions = jnp.concatenate(
         [span_offsets[my_group] + jnp.arange(SPAN, dtype=jnp.int32), own_lengths]
@@ -94,43 +100,11 @@
         jnp.bfloat16
     )
     value_rows = raw_v.reshape(rows_group, local_heads, HD)
-    causal = jnp.arange(SPAN)[:, None] >= jnp.arange(SPAN)[None, :]
-    self_scores = (
-        jnp.einsum(
-            "qhd,khd->qhk", query[:SPAN], key_rows[:SPAN], preferred_element_type=jnp.float32
-        )
-        * score_scale
-    )
-    self_top, self_total, self_numerator = softmax_part(
-        self_scores, causal[:, None, :], value_rows[:SPAN], "qhk,khd->qhd"
-    )
-    own_scores = (
-        jnp.sum(query[SPAN:].astype(jnp.float32) * key_rows[SPAN:].astype(jnp.float32), -1)
-        * score_scale
-    )
-    own_total = jnp.ones_like(own_scores)
-    own_numerator = value_rows[SPAN:].astype(jnp.float32)
-    everyone = lax.all_gather(query, "req", axis=0, tiled=True)
-    everyone = everyone.reshape(groups, rows_group, local_heads, HD)
-    pages_here = prefix_keys.shape[1]
-    block_keys = prefix_keys.reshape(groups, pages_here * page_rows, local_heads, HD)
-    block_values = prefix_values.reshape(groups, pages_here * page_rows, local_heads, HD)
-    key_pos = my_group * pages_here * page_rows + jnp.arange(
-        pages_here * page_rows, dtype=jnp.int32
-    )
-    key_mask = key_pos[None, :] < span_offsets[:, None]
-    scores = (
-        jnp.einsum(
-            "gqhd,gkhd->gqhk", everyone[:, :SPAN], block_keys, preferred_element_type=jnp.float32
-        )
-        * score_scale
-    )
-    pre_top, pre_total, pre_numerator = softmax_part(
-        scores, key_mask[:, None, None, :], block_values, "gqhk,gkhd->gqhd"
-    )
+
+    decode_queries = lax.all_gather(query[SPAN:], "req", axis=0, tiled=True)
     live_slot = slot_owner >= 0
     owner_index = jnp.maximum(slot_owner, 0)
-    slot_queries = everyone[:, SPAN:].reshape(requests, local_heads, HD)[owner_index]
+    slot_queries = decode_queries[owner_index]
     slot_keys = key_cache.reshape(key_cache.shape[0], page_rows, local_heads, HD)
     slot_values = value_cache.reshape(value_cache.shape[0], page_rows, local_heads, HD)
     scores = (
@@ -149,37 +123,55 @@
     request_numerator = jnp.einsum(
         "rsh,shd->rhd", factor, numerator, precision=lax.Precision.HIGHEST
     )
-    send_top = jnp.concatenate([pre_top, best_score.reshape(groups, DEC, local_heads)], 1).reshape(
-        groups * rows_group, local_heads
-    )
-    send_total = jnp.concatenate(
-        [pre_total, request_total.reshape(groups, DEC, local_heads)], 1
-    ).reshape(groups * rows_group, local_heads)
-    send_numerator = jnp.concatenate(
-        [pre_numerator, request_numerator.reshape(groups, DEC, local_heads, HD)], 1
-    ).reshape(groups * rows_group, local_heads, HD)
-    back_top, back_total, back_numerator = (
-        lax.all_to_all(send_top, "req", split_axis=0, concat_axis=0, tiled=True),
-        lax.all_to_all(send_total, "req", split_axis=0, concat_axis=0, tiled=True),
-        lax.all_to_all(send_numerator, "req", split_axis=0, concat_axis=0, tiled=True),
-    )
-    local_top = jnp.concatenate([self_top, own_scores], 0)
-    local_total = jnp.concatenate([self_total, own_total], 0)
-    local_numerator = jnp.concatenate([self_numerator, own_numerator], 0)
-    merged = merge_parts(
-        jnp.concatenate([back_top.reshape(groups, rows_group, local_heads), local_top[None]], 0),
-        jnp.concatenate(
-            [back_total.reshape(groups, rows_group, local_heads), local_total[None]], 0
-        ),
-        jnp.concatenate(
-            [back_numerator.reshape(groups, rows_group, local_heads, HD), local_numerator[None]], 0
-        ),
-    )
+    packed = jnp.concatenate(
+        [request_numerator, best_score[..., None], request_total[..., None]], -1
+    )
+    back = lax.all_to_all(packed, "req", split_axis=0, concat_axis=0, tiled=True)
+    back = back.reshape(groups, DEC, local_heads, HD + 2)
+    own_scores = (
+        jnp.sum(query[SPAN:].astype(jnp.float32) * key_rows[SPAN:].astype(jnp.float32), -1)
+        * score_scale
+    )
+    decode_out = merge_parts(
+        jnp.concatenate([back[..., HD], own_scores[None]], 0),
+        jnp.concatenate([back[..., HD + 1], jnp.ones_like(own_scores)[None]], 0),
+        jnp.concatenate([back[..., :HD], value_rows[SPAN:].astype(jnp.float32)[None]], 0),
+    )
+
+    span_query = query[:SPAN]
+    causal = jnp.arange(SPAN)[:, None] >= jnp.arange(SPAN)[None, :]
+    prefix_mask = jnp.arange(prefix_len, dtype=jnp.int32) < span_offsets[my_group]
+    pre_scores = (
+        jnp.einsum("qhd,khd->qhk", span_query, own_keys, preferred_element_type=jnp.float32)
+        * score_scale
+    )
+    self_scores = (
+        jnp.einsum("qhd,khd->qhk", span_query, key_rows[:SPAN], preferred_element_type=jnp.float32)
+        * score_scale
+    )
+    pre_masked = jnp.where(prefix_mask[None, None, :], pre_scores, NEGATIVE)
+    self_masked = jnp.where(causal[:, None, :], self_scores, NEGATIVE)
+    top = jnp.maximum(jnp.max(pre_masked, -1), jnp.max(self_masked, -1))
+    pre_exp = jnp.where(prefix_mask[None, None, :], jnp.exp(pre_masked - top[..., None]), 0.0)
+    self_exp = jnp.where(causal[:, None, :], jnp.exp(self_masked - top[..., None]), 0.0)
+    total = jnp.sum(pre_exp, -1) + jnp.sum(self_exp, -1)
+    span_numerator = jnp.einsum(
+        "qhk,khd->qhd", pre_exp.astype(jnp.bfloat16), own_values, preferred_element_type=jnp.float32
+    ) + jnp.einsum(
+        "qhk,khd->qhd",
+        self_exp.astype(jnp.bfloat16),
+        value_rows[:SPAN],
+        preferred_element_type=jnp.float32,
+    )
+    span_out = span_numerator / total[..., None]
+
+    merged = jnp.concatenate([span_out, decode_out], 0)
     attention = merged.reshape(rows_group, local_width).astype(jnp.bfloat16)
     share_width = post_gain.shape[0]
-    projected = lax.psum(jnp.dot(attention, out_weight, preferred_element_type=jnp.float32), "tp")
-    inverse = lax.rsqrt(jnp.mean(projected * projected, 1) + EPSILON)
-    my_share = lax.dynamic_slice_in_dim(projected, tp_index * share_width, share_width, 1)
+    partial = jnp.dot(attention, out_weight, preferred_element_type=jnp.float32)
+    my_share = lax.psum_scatter(partial, "tp", scatter_dimension=1, tiled=True)
+    power = lax.psum(jnp.sum(my_share * my_share, 1), "tp")
+    inverse = lax.rsqrt(power / (share_width * tp_count) + EPSILON)
     normed = my_share * inverse[:, None]
     return (hidden.astype(jnp.float32) + normed * post_gain[None, :]).astype(jnp.bfloat16)
 

time: 843 us -> 329 us (0.39)
  waiting for transfers between devices: 633 us -> 66.1 us
  blocking collectives: 15 us -> 149 us
  local copies, waits for them, and re-layouts: 75.1 us -> 33.2 us
  other arithmetic: 46.9 us -> 29.4 us
  starting transfers between devices: 24.5 us -> 7.35 us
    all_to_all x3 -> x1, waiting for transfers between devices: 450 us -> 9.42 us  [body(): lax.all_to_all(prefix_values, 'req', split_axis=0, concat_axis=1, tiled=T...]
    psum x1 -> x0, waiting for transfers between devices: 102 us -> none  [body(): lax.psum(jnp.dot(attention, out_weight, preferred_element_type=jnp.float3...]
    all_to_all x0 -> x2, blocking collectives: none -> 82.1 us  [the longest x1 64.8 us: body(): lax.all_to_all(prefix_keys, 'req', split_axis=0, concat_axis=1, tiled=True)]
    all_gather x1 -> x0, waiting for transfers between devices: 81.2 us -> none  [body(): everyone = lax.all_gather(query, 'req', axis=0, tiled=True)]
    reduce_scatter x0 -> x1, waiting for transfers between devices: none -> 56.7 us  [body(): my_share = lax.psum_scatter(partial, 'tp', scatter_dimension=1, tiled=True)]
    all_gather x0 -> x1, blocking collectives: none -> 38.9 us  [body(): decode_queries = lax.all_gather(query[SPAN:], 'req', axis=0, tiled=True)]
    reshape x8 -> x2, local copies, waits for them, and re-layouts: 45.2 us -> 13.1 us  [the longest x1 9.21 us: body(): own_keys = own_keys.reshape(prefix_len, local_heads, HD)]
    all_to_all x3 -> x1, starting transfers between devices: 24.3 us -> 7.3 us  [body(): lax.all_to_all(prefix_values, 'req', split_axis=0, concat_axis=1, tiled=T...]
  transfers between devices with their start and end apart: 5 -> 2, of which waited for: 3 -> 2; matrix products, arithmetic and copies ran while one was open for 11% -> 15% of each run, Pallas kernels for 0% -> 0%
where the time goes in v1:
time: 329 us; the launch traced here: 327 us
  blocking collectives  149 us (45%)
  waiting for transfers between devices  66.1 us (20%)
  local copies, waits for them, and re-layouts  33.2 us (10%)
  other arithmetic  29.4 us (9%)
  matrix products  28.3 us (9%)
  between operations  13.7 us (4%)
  starting transfers between devices  7.35 us (2%)
    all_to_all x1, blocking collectives, body(): lax.all_to_all(prefix_keys, 'req', split_axis=0, concat_axis=1, tiled=True)  64.8 us
    reduce_scatter x1, waiting for transfers between devices, body(): my_share = lax.psum_scatter(partial, 'tp', scatter_dimension=1, tiled=True)  56.7 us
    all_gather x1, blocking collectives, body(): decode_queries = lax.all_gather(query[SPAN:], 'req', axis=0, tiled=True)  38.9 us
    all_to_all x1, blocking collectives, body(): lax.all_to_all(packed, 'req', split_axis=0, concat_axis=0, tiled=True)  17.3 us
    psum x1, blocking collectives, body(): lax.psum((jnp.sum(float_query * float_query, 1), jnp.sum(float_key * floa...  15 us
    psum x1, blocking collectives, body(): power = lax.psum(jnp.sum(my_share * my_share, 1), 'tp')  13.1 us
    dot_general x1, matrix products, body(): jnp.einsum('qhd,khd->qhk', span_query, own_keys, preferred_element_type=j...  9.94 us
    unnamed x32, local copies, waits for them, and re-layouts  9.72 us
  transfers between devices with their start and end apart: 2, of which 2 were waited for; matrix products, arithmetic and copies ran while one was open for 15% of the time, Pallas kernels for 0%

profile of v1, /device:TPU:1, one launch (start us, length us, event | category | flops | bytes accessed | tf_op | source)
XLA Modules:
  0.0 327.1 jit_solution(14584163546658143109)
XLA Ops:
  6.6 0.7 broadcast_maximum_fusion
  7.3 0.7 broadcast_compare_fusion
  7.9 0.7 iota_compare_fusion.2
  8.6 1.6 copy.111
  10.2 1.1 fusion.22
  11.3 1.1 fusion.24
  12.4 15.0 %all-reduce.1 = (f32[296]{0:T(512)S(1)}, f32[296]{0:T(512)S(1)}) all-reduce(f32[296]{0:T(512)S(1)} %fusion.22, f32[296]{0:T(512)S(1)} %fusion.24), channel_id=1, replica_groups=mesh['req'=32,'tp'=8] {'tp'}, use_global_device_ids=true, to_apply=%region_1.0 | all-reduce | flops 592 | bytes 4736 | tf_op jit(solution)/shard_map/psum | solution.py:88
  27.4 1.1 fusion.23
  29.1 0.6 dynamic_slice.7
  29.7 0.6 iota_add_fusion
  30.7 1.2 fusion.70
  32.1 0.6 multiply_cosine_fusion
  32.7 1.3 subtract_convert_fusion.1
  34.0 0.7 copy-done.5
  34.8 38.9 %all_gather.3 = bf16[256,3,128]{2,0,1:T(8,128)(2,1)S(1)} all-gather(bf16[8,3,128]{2,0,1:T(8,128)(2,1)S(1)} %get-tuple-element.10), channel_id=1, replica_groups=mesh['req'=32,'tp'=8] {'req'}, dimensions={0}, use_global_device_ids=true | all-gather | bytes 202752 | tf_op jit(solution)/shard_map/all_gather | solution.py:104
  73.9 0.6 gather_fusion
  74.5 0.6 gather_fusion.1
  76.2 1.5 copy.112
  78.2 0.6 convolution_bitcast_fusion
  79.2 1.3 reshape.274
  80.5 17.3 %all_to_all.23 = f32[32,1,3120]{2,1,0:T(1,128)} all-to-all(f32[32,1,3120]{2,1,0:T(1,128)S(1)} %reshape.274), channel_id=1, replica_groups=mesh['req'=32,'tp'=8] {'req'}, dimensions={0} | all-to-all | bytes 798720 | tf_op jit(solution)/shard_map/all_to_all | solution.py:129
  97.9 64.8 %all_to_all.24 = bf16[32,1,128,384]{3,2,1,0:T(8,128)(2,1)} all-to-all(bf16[32,1,128,384]{3,2,1,0:T(8,128)(2,1)} %param.24), channel_id=1, replica_groups=mesh['req'=32,'tp'=8] {'req'}, dimensions={0} | all-to-all | bytes 6291456 | tf_op jit(solution)/shard_map/all_to_all | solution.py:76
  162.6 7.3 %all-to-all-start.1 = ((bf16[32,1,128,384]{3,2,1,0:T(8,128)(2,1)}), bf16[32,1,128,384]{3,2,1,0:T(8,128)(2,1)S(1)}, u32[]{:S(2)}, u32[]{:S(2)}) async-start(bf16[32,1,128,384]{3,2,1,0:T(8,128)(2,1)} %param.25), calls=%async_computation.1 | async-start | bytes 6291456 | tf_op jit(solution)/shard_map/all_to_all | solution.py:77
  170.0 0.6 iota_compare_fusion.1
  170.6 1.3 bitcast_convert_fusion
  171.9 3.3 %fusion.71 = (f32[288,3]{0,1:T(4,128)}, f32[288,3,288]{0,2,1:T(8,128)}) fusion(bf16[296,3,64]{2,0,1:T(8,128)(2,1)S(1)} %get-tuple-element.11, bf16[296,3,64]{2,0,1:T(8,128)(2,1)} %copy-done.2, bf16[296,3,64]{2,0,1:T(8,128)(2,1)} %copy-done.5, bf16[296,3,64]{2,0,1:T(8,128)(2,1)} %copy-done.4, pred[288,288]{0,1:T(8,128)(4,1)S(1)} %iota_compare_fusion), kind=kOutput, calls=%fused_computation.124 | convolution fusion | flops 65331360 | bytes 1536384 | tf_op jit(solution)/shard_map/qhd,khd->qhk/dot_general | solution.py:149
  175.7 3.3 %reduce.3 = f32[32,3120]{1,0:T(8,128)} reduce(f32[32,1,3120]{2,1,0:T(1,128)} %all_to_all.23, f32[]{:T(128)} %broadcast.170), dimensions={1}, to_apply=%all_to_all.8.reduce_sub_computation | reduce | bytes 798724 | tf_op jit(solution)/shard_map/all_to_all | solution.py:129
  179.0 3.3 %reshape.275 = f32[256,3,130]{2,1,0:T(4,128)} reshape(f32[32,3120]{1,0:T(8,128)} %reduce.3) | data formatting | bytes 798720
  182.3 1.4 copy.184
  183.7 0.8 slice.71
  184.5 1.0 fusion.68
  185.5 1.2 copy.118
  186.8 1.2 copy.115
  188.0 0.7 multiply_reduce_fusion.1
  188.7 0.8 copy.117
  189.5 1.2 fusion.26
  190.8 9.2 %reshape.272 = bf16[4096,3,128]{2,1,0:T(4,128)(2,1)} reshape(bf16[32,1,128,384]{3,2,1,0:T(8,128)(2,1)} %all_to_all.24) | data formatting | bytes 6291456 | tf_op jit(solution)/shard_map/reshape | solution.py:79
  200.0 9.9 %bitcast_reduce_fusion = (f32[288,3]{0,1:T(4,128)S(1)}, f32[3,288,4096]{2,1,0:T(8,128)}) fusion(pred[4096]{0:T(1024)(128)(4,1)S(1)} %iota_compare_fusion.1, bf16[4096,3,128]{2,1,0:T(4,128)(2,1)} %reshape.272, bf16[296,3,64]{2,0,1:T(8,128)(2,1)S(1)} %get-tuple-element.11, bf16[296,3,64]{2,0,1:T(8,128)(2,1)} %copy-done.2), kind=kOutput, calls=%fused_computation.3 | convolution fusion | flops 917027968 | bytes 17536384 | tf_op jit(solution)/shard_map/qhd,khd->qhk/dot_general | solution.py:145
  210.0 8.9 %fusion.2 = f32[288,3]{0,1:T(4,128)S(1)} fusion(f32[3,288,4096]{2,1,0:T(8,128)} %get-tuple-element.31, f32[288,3]{0,1:T(4,128)S(1)} %max.10, pred[4096]{0:T(1024)(128)(4,1)S(1)} %iota_compare_fusion.1), kind=kLoop, calls=%fused_computation.7 | loop fusion | flops 17693856 | bytes 14166784 | tf_op jit(solution)/shard_map/reduce_sum | solution.py:157
  218.8 9.4 %all-to-all-done.1 = bf16[32,1,128,384]{3,2,1,0:T(8,128)(2,1)S(1)} async-done(((bf16[32,1,128,384]{3,2,1,0:T(8,128)(2,1)}), bf16[32,1,128,384]{3,2,1,0:T(8,128)(2,1)S(1)}, u32[]{:S(2)}, u32[]{:S(2)}) %all-to-all-start.1) | async-done | bytes 3145760 | tf_op jit(solution)/shard_map/all_to_all | solution.py:77
  228.3 3.9 %reshape.273 = bf16[4096,3,128]{2,1,0:T(4,128)(2,1)} reshape(bf16[32,1,128,384]{3,2,1,0:T(8,128)(2,1)S(1)} %all-to-all-done.1) | data formatting | bytes 6291456 | tf_op jit(solution)/shard_map/reshape | solution.py:80
  232.1 8.6 %fusion.4 = f32[3,288,128]{2,1,0:T(8,128)S(1)} fusion(f32[3,288,4096]{2,1,0:T(8,128)} %get-tuple-element.31, f32[288,3]{0,1:T(4,128)S(1)} %max.10, pred[4096]{0:T(1024)(128)(4,1)S(1)} %iota_compare_fusion.1, bf16[4096,3,128]{2,1,0:T(4,128)(2,1)} %reshape.273), kind=kOutput, calls=%fused_computation.9 | convolution fusion | flops 923664384 | bytes 17751424 | tf_op jit(solution)/shard_map/qhk,khd->qhd/dot_general | solution.py:158
  241.6 1.3 copy-done.1
  242.8 4.4 %fusion.27 = f32[296,5120]{1,0:T(8,128)} fusion(bf16[384,5120]{1,0:T(8,128)(2,1)S(1)} %copy-done.1, bf16[8,3,128]{2,0,1:T(8,128)(2,1)S(1)} %divide_convert_fusion, bf16[288,3,128]{2,0,1:T(8,128)(2,1)S(1)} %fusion.15), kind=kOutput, calls=%fused_computation.48 | convolution fusion | flops 1164374016 | bytes 10221568 | tf_op jit(solution)/shard_map/dot_general | solution.py:171
  247.2 56.7 %reduce-scatter.2.cloned.1.call-done = f32[296,640]{1,0:T(8,128)} async-done(((f32[296,5120]{1,0:T(8,128)}), f32[296,640]{1,0:T(8,128)}) %reduce-scatter.2.cloned.1.call-update) | async-done | bytes 757776 | tf_op jit(solution)/shard_map/reduce_scatter | solution.py:172
  303.9 1.3 multiply_reduce_fusion
  305.2 13.1 %psum.23 = f32[296]{0:T(512)S(1)} all-reduce(f32[296]{0:T(512)S(1)} %multiply_reduce_fusion), channel_id=1, replica_groups=mesh['req'=32,'tp'=8] {'tp'}, use_global_device_ids=true, to_apply=%region_17.18 | all-reduce | flops 296 | bytes 2368 | tf_op jit(solution)/shard_map/psum | solution.py:173
  318.2 2.1 add_convert_fusion
  (62 shorter events, 4.9 us)
Async XLA Ops:
  6.5 23.8 %copy-start.6 = (bf16[296,384]{1,0:T(8,128)(2,1)S(1)}, bf16[296,384]{1,0:T(8,128)(2,1)}, u32[]{:S(2)}) copy-start(bf16[296,384]{1,0:T(8,128)(2,1)} %param.18) | copy-start | bytes 681988
  6.5 22.5 %copy-start.12 = (s32[32]{0:T(128)S(1)}, s32[32]{0:T(128)}, u32[]{:S(2)}) copy-start(s32[32]{0:T(128)} %param.31) | copy-start | bytes 388
  6.5 23.8 %copy-start.10 = (f32[384]{0:T(512)S(1)}, f32[384]{0:T(512)}, u32[]{:S(2)}) copy-start(f32[384]{0:T(512)} %param.21) | copy-start | bytes 4612
  12.4 19.5 %copy-start = (s32[256]{0:T(256)S(1)}, s32[256]{0:T(256)}, u32[]{:S(2)}) copy-start(s32[256]{0:T(256)} %param.30) | copy-start | bytes 3076
  30.7 44.4 %copy-start.13 = (s32[8]{0:T(128)S(1)}, s32[8]{0:T(128)}, u32[]{:S(2)}) copy-start(s32[8]{0:T(128)} %param.29) | copy-start | bytes 100
  34.0 0.7 copy-start.5
  34.0 42.2 %copy-start.2 = (bf16[296,3,64]{2,0,1:T(8,128)(2,1)}, bf16[296,3,64]{2,0,1:T(8,128)(2,1)S(1)}, u32[]{:S(2)}) copy-start(bf16[296,3,64]{2,0,1:T(8,128)(2,1)S(1)} %get-tuple-element.12) | copy-start | bytes 340996
  34.0 42.1 %copy-start.4 = (bf16[296,3,64]{2,0,1:T(8,128)(2,1)}, bf16[296,3,64]{2,0,1:T(8,128)(2,1)S(1)}, u32[]{:S(2)}) copy-start(bf16[296,3,64]{2,0,1:T(8,128)(2,1)S(1)} %get-tuple-element.22) | copy-start | bytes 340996
  162.6 65.6 %all-to-all-start.1 = ((bf16[32,1,128,384]{3,2,1,0:T(8,128)(2,1)}), bf16[32,1,128,384]{3,2,1,0:T(8,128)(2,1)S(1)}, u32[]{:S(2)}, u32[]{:S(2)}) async-start(bf16[32,1,128,384]{3,2,1,0:T(8,128)(2,1)} %param.25), calls=%async_computation.1 | async-start | bytes 6291456 | tf_op jit(solution)/shard_map/all_to_all | solution.py:77
  169.9 134.0 %reduce-scatter.2.cloned.1.call-start = ((), (), s32[]{:S(2)}) async-start(), calls=%async_computation.4 | async-start | bytes 6819840 | tf_op jit(solution)/shard_map/reduce_scatter | solution.py:172
  200.0 9.9 %copy-start.8 = (f32[288,3]{0,1:T(4,128)S(1)}, f32[288,3]{0,1:T(4,128)}, u32[]{:S(2)}) copy-start(f32[288,3]{0,1:T(4,128)} %get-tuple-element.32) | copy-start | bytes 10372
  232.1 8.6 %copy-start.3 = (f32[288,3,288]{0,2,1:T(8,128)S(1)}, f32[288,3,288]{0,2,1:T(8,128)}, u32[]{:S(2)}) copy-start(f32[288,3,288]{0,2,1:T(8,128)} %get-tuple-element.33) | copy-start | bytes 2985988
  232.1 8.9 %copy-start.11 = (bf16[296,384]{1,0:T(8,128)(2,1)S(1)}, bf16[296,384]{1,0:T(8,128)(2,1)}, u32[]{:S(2)}) copy-start(bf16[296,384]{1,0:T(8,128)(2,1)} %param.19) | copy-start | bytes 681988
  240.7 2.1 copy-start.1
  247.2 71.1 %copy-start.7 = (bf16[296,640]{1,0:T(8,128)(2,1)S(1)}, bf16[296,640]{1,0:T(8,128)(2,1)}, u32[]{:S(2)}) copy-start(bf16[296,640]{1,0:T(8,128)(2,1)} %param.16) | copy-start | bytes 1136644
  247.2 71.1 %copy-start.9 = (f32[640]{0:T(1024)S(1)}, f32[640]{0:T(1024)}, u32[]{:S(2)}) copy-start(f32[640]{0:T(1024)} %param.23) | copy-start | bytes 7684
Sparse Core Ops, SparseCore 0:
  247.3 56.4 reduce-scatter.1

commit v2 on v1

--- a/solution.py
+++ b/solution.py
@@ -73,11 +73,13 @@
     score_scale = HD ** (-0.5)
     page_rows = key_cache.shape[1]
 
-    own_keys = lax.all_to_all(prefix_keys, "req", split_axis=0, concat_axis=1, tiled=True)
-    own_values = lax.all_to_all(prefix_values, "req", split_axis=0, concat_axis=1, tiled=True)
-    prefix_len = own_keys.shape[1] * page_rows
-    own_keys = own_keys.reshape(prefix_len, local_heads, HD)
-    own_values = own_values.reshape(prefix_len, local_heads, HD)
+    pages_here = prefix_keys.shape[1]
+    both = jnp.concatenate([prefix_keys, prefix_values], 1)
+    both = lax.all_to_all(both, "req", split_axis=0, concat_axis=1, tiled=True)
+    both = both.reshape(groups, 2, pages_here, page_rows, local_heads, HD)
+    prefix_len = groups * pages_here * page_rows
+    own_keys = both[:, 0].reshape(prefix_len, local_heads, HD)
+    own_values = both[:, 1].reshape(prefix_len, local_heads, HD)
 
     own_lengths = lax.dynamic_slice_in_dim(cache_lengths, my_group * DEC, DEC)
     positions = jnp.concatenate(
@@ -101,7 +103,10 @@
     )
     value_rows = raw_v.reshape(rows_group, local_heads, HD)
 
-    decode_queries = lax.all_gather(query[SPAN:], "req", axis=0, tiled=True)
+    placed = lax.dynamic_update_slice_in_dim(
+        jnp.zeros((requests, local_heads, HD), jnp.bfloat16), query[SPAN:], my_group * DEC, 0
+    )
+    decode_queries = lax.psum(placed, "req")
     live_slot = slot_owner >= 0
     owner_index = jnp.maximum(slot_owner, 0)
     slot_queries = decode_queries[owner_index]

time: 329 us -> 455 us (1.38)
  waiting for transfers between devices: 66.1 us -> 311 us
  blocking collectives: 149 us -> 28.1 us
  starting transfers between devices: 7.35 us -> 14.3 us
  matrix products: 28.3 us -> 23.3 us
    psum x0 -> x1, waiting for transfers between devices: none -> 140 us  [body(): decode_queries = lax.psum(placed, 'req')]
    all_to_all x1 -> x2, waiting for transfers between devices: 9.42 us -> 123 us  [the longest x1 123 us: body(): both = lax.all_to_all(both, 'req', split_axis=0, concat_axis=1, tiled=True)]
    all_to_all x2 -> x0, blocking collectives: 82.1 us -> none  [the longest x1 64.8 us: body(): lax.all_to_all(prefix_keys, 'req', split_axis=0, concat_axis=1, tiled=True)]
    all_gather x1 -> x0, blocking collectives: 38.9 us -> none  [body(): decode_queries = lax.all_gather(query[SPAN:], 'req', axis=0, tiled=True)]
    reshape x2 -> x0, local copies, waits for them, and re-layouts: 13.1 us -> none  [the longest x1 9.21 us: body(): own_keys = own_keys.reshape(prefix_len, local_heads, HD)]
    slice x0 -> x3, local copies, waits for them, and re-layouts: none -> 12.8 us  [the longest x2 10 us: body(): own_keys = both[:, 0].reshape(prefix_len, local_heads, HD)]
    reduce_scatter x1, waiting for transfers between devices: 56.7 us -> 48.9 us  [body(): my_share = lax.psum_scatter(partial, 'tp', scatter_dimension=1, tiled=True)]
    all_to_all x1 -> x2, starting transfers between devices: 7.3 us -> 14 us  [the longest x1 9.41 us: body(): both = lax.all_to_all(both, 'req', split_axis=0, concat_axis=1, tiled=True)]
  transfers between devices with their start and end apart: 2 -> 4, of which waited for: 2 -> 3; matrix products, arithmetic and copies ran while one was open for 15% -> 6% of each run, Pallas kernels for 0% -> 0%
where the time goes in v2:
time: 455 us; the launch traced here: 454 us
  waiting for transfers between devices  311 us (68%)
  local copies, waits for them, and re-layouts  34.8 us (8%)
  other arithmetic  28.2 us (6%)
  blocking collectives  28.1 us (6%)
  matrix products  23.3 us (5%)
  starting transfers between devices  14.3 us (3%)
  between operations  13.9 us (3%)
    psum x1, waiting for transfers between devices, body(): decode_queries = lax.psum(placed, 'req')  140 us
    all_to_all x1, waiting for transfers between devices, body(): both = lax.all_to_all(both, 'req', split_axis=0, concat_axis=1, tiled=True)  123 us
    reduce_scatter x1, waiting for transfers between devices, body(): my_share = lax.psum_scatter(partial, 'tp', scatter_dimension=1, tiled=True)  48.9 us
    unnamed x46, local copies, waits for them, and re-layouts  16.1 us
    psum x1, blocking collectives, body(): lax.psum((jnp.sum(float_query * float_query, 1), jnp.sum(float_key * floa...  15 us
    psum x1, blocking collectives, body(): power = lax.psum(jnp.sum(my_share * my_share, 1), 'tp')  13.1 us
    slice x2, local copies, waits for them, and re-layouts, body(): own_keys = both[:, 0].reshape(prefix_len, local_heads, HD)  10 us
    all_to_all x1, starting transfers between devices, body(): both = lax.all_to_all(both, 'req', split_axis=0, concat_axis=1, tiled=True)  9.41 us
  transfers between devices with their start and end apart: 4, of which 3 were waited for; matrix products, arithmetic and copies ran while one was open for 6% of the time, Pallas kernels for 0%

profile of v2, /device:TPU:1, one launch (start us, length us, event | category | flops | bytes accessed | tf_op | source)
XLA Modules:
  0.0 453.8 jit_solution(17722241259432662613)
XLA Ops:
  6.6 1.1 fusion.22
  7.7 1.1 fusion.24
  8.8 15.0 %all-reduce.1 = (f32[296]{0:T(512)S(1)}, f32[296]{0:T(512)S(1)}) all-reduce(f32[296]{0:T(512)S(1)} %fusion.22, f32[296]{0:T(512)S(1)} %fusion.24), channel_id=1, replica_groups=mesh['req'=32,'tp'=8] {'tp'}, use_global_device_ids=true, to_apply=%region_1.0 | all-reduce | flops 592 | bytes 4736 | tf_op jit(solution)/shard_map/psum | solution.py:90
  23.8 1.0 fusion.23
  25.0 0.4 fusion.71
  25.4 0.7 dynamic_slice.7
  26.1 0.7 iota_add_fusion
  27.1 0.4 fusion.72
  27.7 0.6 multiply_cosine_fusion
  28.3 0.2 subtract_convert_fusion.1
  28.8 0.5 copy-done.9
  29.4 0.7 copy-done.6
  30.2 1.5 copy.113
  31.7 0.6 gather_fusion
  32.4 0.4 copy.114
  32.9 139.6 %all-reduce.4.cloned.1.call-done = bf16[256,3,128]{2,1,0:T(4,128)(2,1)} async-done(((bf16[256,3,128]{2,1,0:T(4,128)(2,1)}), bf16[256,3,128]{2,1,0:T(4,128)(2,1)}) %all-reduce.4.cloned.1.call-update) | async-done | bytes 196624 | tf_op jit(solution)/shard_map/psum | solution.py:109
  172.5 1.5 gather_fusion.1
  174.0 0.3 fusion.42
  174.9 0.5 fusion.40
  175.4 0.6 convolution_bitcast_fusion.1
  176.1 0.4 copy.115
  176.5 2.1 reshape.264
  178.6 4.6 %all-to-all-start.1 = ((f32[32,1,3120]{2,1,0:T(1,128)}), f32[32,1,3120]{2,1,0:T(1,128)}, u32[]{:S(2)}, u32[]{:S(2)}) async-start(f32[32,1,3120]{2,1,0:T(1,128)} %reshape.264), calls=%async_computation.1 | async-start | bytes 819200 | tf_op jit(solution)/shard_map/all_to_all | solution.py:134
  183.2 3.5 copy.103
  186.7 4.7 %copy.102 = bf16[32,1,128,384]{2,3,1,0:T(8,128)(2,1)} copy(bf16[32,1,128,384]{3,2,1,0:T(8,128)(2,1)} %param.24) | data formatting | bytes 6291456 | tf_op args[8]
  191.4 5.1 %pad_maximum_fusion = bf16[32,2,128,384]{2,3,1,0:T(8,128)(2,1)} fusion(bf16[32,1,128,384]{2,3,1,0:T(8,128)(2,1)S(1)} %copy.103, bf16[32,1,128,384]{2,3,1,0:T(8,128)(2,1)} %copy.102), kind=kLoop, calls=%fused_computation.12 | loop fusion | flops 3145728 | bytes 12582912 | tf_op jit(solution)/shard_map/concatenate | solution.py:77
  196.6 9.4 %all-to-all-start = ((bf16[32,2,128,384]{2,3,1,0:T(8,128)(2,1)}), bf16[32,2,128,384]{2,3,1,0:T(8,128)(2,1)}, u32[]{:S(2)}, u32[]{:S(2)}) async-start(bf16[32,2,128,384]{2,3,1,0:T(8,128)(2,1)} %pad_maximum_fusion), calls=%async_computation | async-start | bytes 12582912 | tf_op jit(solution)/shard_map/all_to_all | solution.py:78
  206.2 0.7 iota_compare_fusion.1
  206.9 0.7 bitcast_convert_fusion
  207.6 1.6 fusion.73
  209.2 0.5 broadcast.170
  209.7 2.6 reduce.3
  212.3 1.3 reshape.265
  215.2 122.8 %all-to-all-done = bf16[32,2,128,384]{2,3,1,0:T(8,128)(2,1)} async-done(((bf16[32,2,128,384]{2,3,1,0:T(8,128)(2,1)}), bf16[32,2,128,384]{2,3,1,0:T(8,128)(2,1)}, u32[]{:S(2)}, u32[]{:S(2)}) %all-to-all-start) | async-done | bytes 6291488 | tf_op jit(solution)/shard_map/all_to_all | solution.py:78
  338.0 6.5 %fusion.69 = (bf16[32,1,1,128,3,128]{3,5,4,1,0,2:T(8,128)(2,1)}, bf16[32,1,1,128,3,128]{3,5,4,1,0,2:T(8,128)(2,1)S(1)}) fusion(bf16[32,2,1,128,3,128]{3,5,4,1,0,2:T(8,128)(2,1)} %bitcast), kind=kLoop, calls=%fused_computation.122 | loop fusion | bytes 12582912 | tf_op jit(solution)/shard_map/slice | solution.py:81
  344.6 2.8 copy.104
  347.4 3.5 copy.105
  350.9 8.3 %bitcast_reduce_fusion = (f32[288,3]{0,1:T(4,128)S(1)}, f32[3,4096,288]{1,2,0:T(8,128)}) fusion(pred[4096]{0:T(1024)(128)(4,1)S(1)} %iota_compare_fusion.1, bf16[4096,3,128]{2,0,1:T(8,128)(2,1)S(1)} %bitcast.93, bf16[296,3,64]{2,0,1:T(8,128)(2,1)S(1)} %get-tuple-element.13, bf16[296,3,64]{2,0,1:T(8,128)(2,1)} %copy-done.3), kind=kOutput, calls=%fused_computation.3 | convolution fusion | flops 917027968 | bytes 17536384 | tf_op jit(solution)/shard_map/qhd,khd->qhk/dot_general | solution.py:150
  359.2 9.0 %fusion.2 = f32[288,3]{0,1:T(4,128)S(1)} fusion(f32[3,4096,288]{1,2,0:T(8,128)} %get-tuple-element.33, f32[288,3]{0,1:T(4,128)S(1)} %max.10, pred[4096]{0:T(1024)(128)(4,1)S(1)} %iota_compare_fusion.1), kind=kLoop, calls=%fused_computation.7 | loop fusion | flops 17693856 | bytes 14166784 | tf_op jit(solution)/shard_map/reduce_sum | solution.py:162
  368.2 7.0 %fusion.12 = f32[288,3,128]{2,0,1:T(8,128)S(1)} fusion(bf16[4096,3,128]{2,0,1:T(8,128)(2,1)S(1)} %bitcast.96, f32[3,4096,288]{1,2,0:T(8,128)} %get-tuple-element.33, f32[288,3]{0,1:T(4,128)S(1)} %max.10, pred[4096]{0:T(1024)(128)(4,1)S(1)} %iota_compare_fusion.1), kind=kOutput, calls=%fused_computation.20 | convolution fusion | flops 923664384 | bytes 17751424 | tf_op jit(solution)/shard_map/qhk,khd->qhd/dot_general | solution.py:163
  375.2 0.3 fusion.16
  375.5 0.6 fusion.15
  376.1 1.2 copy-done.1
  377.3 4.4 fusion.27
  381.7 48.9 %reduce-scatter.2.cloned.1.call-done = f32[296,640]{1,0:T(8,128)} async-done(((f32[296,5120]{1,0:T(8,128)}), f32[296,640]{1,0:T(8,128)}) %reduce-scatter.2.cloned.1.call-update) | async-done | bytes 757776 | tf_op jit(solution)/shard_map/reduce_scatter | solution.py:177
  430.5 1.3 multiply_reduce_fusion
  431.8 13.1 %psum.31 = f32[296]{0:T(512)S(1)} all-reduce(f32[296]{0:T(512)S(1)} %multiply_reduce_fusion), channel_id=1, replica_groups=mesh['req'=32,'tp'=8] {'tp'}, use_global_device_ids=true, to_apply=%region_18.19 | all-reduce | flops 296 | bytes 2368 | tf_op jit(solution)/shard_map/psum | solution.py:178
  444.9 2.1 add_convert_fusion
  (81 shorter events, 3.6 us)
Async XLA Ops:
  6.5 20.3 %copy-start.11 = (bf16[296,384]{1,0:T(8,128)(2,1)S(1)}, bf16[296,384]{1,0:T(8,128)(2,1)}, u32[]{:S(2)}) copy-start(bf16[296,384]{1,0:T(8,128)(2,1)} %param.18) | copy-start | bytes 681988
  6.5 18.9 %copy-start.18 = (s32[32]{0:T(128)S(1)}, s32[32]{0:T(128)}, u32[]{:S(2)}) copy-start(s32[32]{0:T(128)} %param.31) | copy-start | bytes 388
  6.5 20.3 %copy-start.15 = (f32[384]{0:T(512)S(1)}, f32[384]{0:T(512)}, u32[]{:S(2)}) copy-start(f32[384]{0:T(512)} %param.21) | copy-start | bytes 4612
  6.5 165.9 %all-reduce.4.cloned.1.call-start = ((), (), s32[]{:S(2)}) async-start(), calls=%async_computation.3 | async-start | bytes 524288 | tf_op jit(solution)/shard_map/psum | solution.py:109
  25.0 2.5 copy-start
  27.1 3.0 copy-start.16
  28.3 4.1 copy-start.19
  28.6 0.7 copy-start.9
  28.6 3.8 copy-start.3
  28.6 3.8 copy-start.7
  28.6 3.8 copy-start.12
  29.4 0.7 copy-start.6
  178.6 18.0 %all-to-all-start.1 = ((f32[32,1,3120]{2,1,0:T(1,128)}), f32[32,1,3120]{2,1,0:T(1,128)}, u32[]{:S(2)}, u32[]{:S(2)}) async-start(f32[32,1,3120]{2,1,0:T(1,128)} %reshape.264), calls=%async_computation.1 | async-start | bytes 819200 | tf_op jit(solution)/shard_map/all_to_all | solution.py:134
  196.6 11.1 %copy-start.4 = (bf16[296,3,64]{2,0,1:T(8,128)(2,1)S(1)}, bf16[296,3,64]{2,0,1:T(8,128)(2,1)}, u32[]{:S(2)}) copy-start(bf16[296,3,64]{2,0,1:T(8,128)(2,1)} %copy-done.3) | copy-start | bytes 340996
  196.6 11.1 %copy-start.8 = (bf16[296,3,64]{2,0,1:T(8,128)(2,1)S(1)}, bf16[296,3,64]{2,0,1:T(8,128)(2,1)}, u32[]{:S(2)}) copy-start(bf16[296,3,64]{2,0,1:T(8,128)(2,1)} %copy-done.7) | copy-start | bytes 340996
  196.6 11.1 %copy-start.10 = (bf16[296,3,64]{2,0,1:T(8,128)(2,1)S(1)}, bf16[296,3,64]{2,0,1:T(8,128)(2,1)}, u32[]{:S(2)}) copy-start(bf16[296,3,64]{2,0,1:T(8,128)(2,1)} %copy-done.9) | copy-start | bytes 340996
  196.6 141.5 %all-to-all-start = ((bf16[32,2,128,384]{2,3,1,0:T(8,128)(2,1)}), bf16[32,2,128,384]{2,3,1,0:T(8,128)(2,1)}, u32[]{:S(2)}, u32[]{:S(2)}) async-start(bf16[32,2,128,384]{2,3,1,0:T(8,128)(2,1)} %pad_maximum_fusion), calls=%async_computation | async-start | bytes 12582912 | tf_op jit(solution)/shard_map/all_to_all | solution.py:78
  206.0 224.6 %reduce-scatter.2.cloned.1.call-start = ((), (), s32[]{:S(2)}) async-start(), calls=%async_computation.4 | async-start | bytes 6819840 | tf_op jit(solution)/shard_map/reduce_scatter | solution.py:177
  359.2 9.0 %copy-start.2 = (bf16[32,1,1,128,3,128]{5,3,0,4,2,1:T(8,128)(2,1)S(1)}, bf16[32,1,1,128,3,128]{5,3,0,4,2,1:T(8,128)(2,1)}, u32[]{:S(2)}) copy-start(bf16[32,1,1,128,3,128]{5,3,0,4,2,1:T(8,128)(2,1)} %copy.104) | copy-start | bytes 9437188
  368.2 7.0 %copy-start.5 = (f32[288,3,288]{0,2,1:T(8,128)S(1)}, f32[288,3,288]{0,2,1:T(8,128)}, u32[]{:S(2)}) copy-start(f32[288,3,288]{0,2,1:T(8,128)} %get-tuple-element.35) | copy-start | bytes 2985988
  368.2 7.3 %copy-start.17 = (bf16[296,384]{1,0:T(8,128)(2,1)S(1)}, bf16[296,384]{1,0:T(8,128)(2,1)}, u32[]{:S(2)}) copy-start(bf16[296,384]{1,0:T(8,128)(2,1)} %param.19) | copy-start | bytes 681988
  375.2 2.1 copy-start.1
  381.7 63.3 %copy-start.13 = (bf16[296,640]{1,0:T(8,128)(2,1)S(1)}, bf16[296,640]{1,0:T(8,128)(2,1)}, u32[]{:S(2)}) copy-start(bf16[296,640]{1,0:T(8,128)(2,1)} %param.16) | copy-start | bytes 1136644
  381.7 63.3 %copy-start.14 = (f32[640]{0:T(1024)S(1)}, f32[640]{0:T(1024)}, u32[]{:S(2)}) copy-start(f32[640]{0:T(1024)} %param.23) | copy-start | bytes 7684
Sparse Core Ops, SparseCore 0:
  30.2 142.2 all-reduce.3
  381.8 48.6 reduce-scatter.1

commit v3 on v1

--- a/solution.py
+++ b/solution.py
@@ -73,11 +73,6 @@
     score_scale = HD ** (-0.5)
     page_rows = key_cache.shape[1]
 
-    own_keys = lax.all_to_all(prefix_keys, "req", split_axis=0, concat_axis=1, tiled=True)
-    own_values = lax.all_to_all(prefix_values, "req", split_axis=0, concat_axis=1, tiled=True)
-    prefix_len = own_keys.shape[1] * page_rows
-    own_keys = own_keys.reshape(prefix_len, local_heads, HD)
-    own_values = own_values.reshape(prefix_len, local_heads, HD)
 
     own_lengths = lax.dynamic_slice_in_dim(cache_lengths, my_group * DEC, DEC)
     positions = jnp.concatenate(
@@ -101,7 +96,23 @@
     )
     value_rows = raw_v.reshape(rows_group, local_heads, HD)
 
-    decode_queries = lax.all_gather(query[SPAN:], "req", axis=0, tiled=True)
+    pages_here = prefix_keys.shape[1]
+    block_rows = pages_here * page_rows
+    outgoing = jnp.concatenate(
+        [
+            prefix_keys.reshape(groups, block_rows, local_width),
+            prefix_values.reshape(groups, block_rows, local_width),
+            jnp.broadcast_to(
+                query[None, SPAN:].reshape(1, DEC, local_width), (groups, DEC, local_width)
+            ),
+        ],
+        1,
+    )
+    incoming = lax.all_to_all(outgoing, "req", split_axis=0, concat_axis=0, tiled=True)
+    prefix_len = groups * block_rows
+    own_keys = incoming[:, :block_rows].reshape(prefix_len, local_heads, HD)
+    own_values = incoming[:, block_rows : 2 * block_rows].reshape(prefix_len, local_heads, HD)
+    decode_queries = incoming[:, 2 * block_rows :].reshape(requests, local_heads, HD)
     live_slot = slot_owner >= 0
     owner_index = jnp.maximum(slot_owner, 0)
     slot_queries = decode_queries[owner_index]

time: 329 us -> 345 us (1.049)
  waiting for transfers between devices: 66.1 us -> 192 us
  blocking collectives: 149 us -> 28 us
  starting transfers between devices: 7.35 us -> 19.1 us
    all_to_all x1 -> x2, waiting for transfers between devices: 9.42 us -> 135 us  [the longest x1 135 us: body(): lax.all_to_all(outgoing, 'req', split_axis=0, concat_axis=0, tiled=True)]
    all_to_all x2 -> x0, blocking collectives: 82.1 us -> none  [the longest x1 64.8 us: body(): lax.all_to_all(prefix_keys, 'req', split_axis=0, concat_axis=1, tiled=True)]
    all_gather x1 -> x0, blocking collectives: 38.9 us -> none  [body(): decode_queries = lax.all_gather(query[SPAN:], 'req', axis=0, tiled=True)]
    all_to_all x1 -> x2, starting transfers between devices: 7.3 us -> 18.9 us  [the longest x1 9.75 us: body(): lax.all_to_all(outgoing, 'req', split_axis=0, concat_axis=0, tiled=True)]
    slice x0 -> x2, local copies, waits for them, and re-layouts: none -> 6.43 us  [the longest x1 5.49 us: body(): own_keys = incoming[:, :block_rows].reshape(prefix_len, local_heads, HD)]
    concatenate x0 -> x1, other arithmetic: none -> 5.17 us  [body(): jnp.concatenate([prefix_keys.reshape(groups, block_rows, local_width), pr...]
    unnamed x32 -> x42, local copies, waits for them, and re-layouts: 9.72 us -> 6.05 us
    reshape x2 -> x3, local copies, waits for them, and re-layouts: 13.1 us -> 13 us  [the longest x1 9.02 us: body(): incoming[:, block_rows:2 * block_rows].reshape(prefix_len, local_heads, HD)]
  transfers between devices with their start and end apart: 2 -> 3, of which waited for: 2 -> 2; matrix products, arithmetic and copies ran while one was open for 15% -> 15% of each run, Pallas kernels for 0% -> 0%
where the time goes in v3:
time: 345 us; the launch traced here: 343 us
  waiting for transfers between devices  192 us (56%)
  local copies, waits for them, and re-layouts  32.4 us (9%)
  other arithmetic  29.9 us (9%)
  blocking collectives  28 us (8%)
  matrix products  27.7 us (8%)
  starting transfers between devices  19.1 us (6%)
  between operations  13.8 us (4%)
    all_to_all x1, waiting for transfers between devices, body(): lax.all_to_all(outgoing, 'req', split_axis=0, concat_axis=0, tiled=True)  135 us
    reduce_scatter x1, waiting for transfers between devices, body(): my_share = lax.psum_scatter(partial, 'tp', scatter_dimension=1, tiled=True)  57.6 us
    psum x1, blocking collectives, body(): lax.psum((jnp.sum(float_query * float_query, 1), jnp.sum(float_key * floa...  15 us
    psum x1, blocking collectives, body(): power = lax.psum(jnp.sum(my_share * my_share, 1), 'tp')  13.1 us
    dot_general x1, matrix products, body(): jnp.einsum('qhd,khd->qhk', span_query, own_keys, preferred_element_type=j...  10.1 us
    all_to_all x1, starting transfers between devices, body(): lax.all_to_all(outgoing, 'req', split_axis=0, concat_axis=0, tiled=True)  9.75 us
    reduce_sum x2, other arithmetic, body(): total = jnp.sum(pre_exp, -1) + jnp.sum(self_exp, -1)  9.28 us
    all_to_all x1, starting transfers between devices, body(): lax.all_to_all(packed, 'req', split_axis=0, concat_axis=0, tiled=True)  9.17 us
  transfers between devices with their start and end apart: 3, of which 2 were waited for; matrix products, arithmetic and copies ran while one was open for 15% of the time, Pallas kernels for 0%

profile of v3, /device:TPU:1, one launch (start us, length us, event | category | flops | bytes accessed | tf_op | source)
XLA Modules:
  0.0 343.1 jit_solution(16933577239237321265)
XLA Ops:
  6.6 1.1 fusion.27
  7.7 1.1 fusion.29
  8.8 15.0 %all-reduce.1 = (f32[296]{0:T(512)S(1)}, f32[296]{0:T(512)S(1)}) all-reduce(f32[296]{0:T(512)S(1)} %fusion.27, f32[296]{0:T(512)S(1)} %fusion.29), channel_id=1, replica_groups=mesh['req'=32,'tp'=8] {'tp'}, use_global_device_ids=true, to_apply=%region_1.0 | all-reduce | flops 592 | bytes 4736 | tf_op jit(solution)/shard_map/psum | solution.py:83
  23.8 1.1 fusion.28
  25.0 1.4 fusion.75
  26.4 0.6 dynamic_slice.7
  27.1 0.6 iota_add_fusion
  28.0 1.5 fusion.76
  29.6 0.6 multiply_cosine_fusion
  30.2 2.0 subtract_convert_fusion.1
  32.3 0.7 copy-done.3
  33.2 5.2 %pad_maximum_fusion = bf16[32,264,384]{2,1,0:T(8,128)(2,1)} fusion(bf16[32,8,384]{2,1,0:T(8,128)(2,1)S(1)} %broadcast_in_dim.145, bf16[32,128,384]{2,1,0:T(8,128)(2,1)S(1)} %bitcast.95, bf16[32,128,384]{2,1,0:T(8,128)(2,1)} %bitcast.96), kind=kLoop, calls=%fused_computation.12 | loop fusion | flops 19464192 | bytes 12976128 | tf_op jit(solution)/shard_map/concatenate | solution.py:101
  38.4 9.8 %all-to-all-start = ((bf16[32,264,384]{2,1,0:T(8,128)(2,1)}), bf16[32,264,384]{2,1,0:T(8,128)(2,1)}, u32[]{:S(2)}, u32[]{:S(2)}) async-start(bf16[32,264,384]{2,1,0:T(8,128)(2,1)} %pad_maximum_fusion), calls=%async_computation | async-start | bytes 12976128 | tf_op jit(solution)/shard_map/all_to_all | solution.py:111
  48.1 0.4 copy.106
  48.6 0.6 gather_fusion
  49.2 1.5 copy.107
  50.7 0.6 iota_compare_fusion.1
  51.6 0.7 bitcast_convert_fusion
  52.3 1.5 fusion.77
  53.8 134.5 %all-to-all-done = bf16[32,264,384]{2,1,0:T(8,128)(2,1)} async-done(((bf16[32,264,384]{2,1,0:T(8,128)(2,1)}), bf16[32,264,384]{2,1,0:T(8,128)(2,1)}, u32[]{:S(2)}, u32[]{:S(2)}) %all-to-all-start) | async-done | bytes 6488096 | tf_op jit(solution)/shard_map/all_to_all | solution.py:111
  188.3 0.9 slice.84
  189.4 0.6 gather_fusion.1
  189.9 0.3 fusion.47
  190.6 0.2 fusion.40
  190.9 0.5 fusion.45
  191.4 0.6 convolution_bitcast_fusion.1
  192.0 0.4 copy.108
  192.4 2.1 reshape.279
  194.5 9.2 %all-to-all-start.1 = ((f32[32,1,3120]{2,1,0:T(1,128)}), f32[32,1,3120]{2,1,0:T(1,128)}, u32[]{:S(2)}, u32[]{:S(2)}) async-start(f32[32,1,3120]{2,1,0:T(1,128)} %reshape.279), calls=%async_computation.1 | async-start | bytes 819200 | tf_op jit(solution)/shard_map/all_to_all | solution.py:140
  203.7 0.2 reduce-scatter.2.cloned.1.call-start
  203.9 5.5 %fusion.73 = (bf16[32,128,384]{2,1,0:T(8,128)(2,1)S(1)}, bf16[32,128,384]{2,1,0:T(8,128)(2,1)}) fusion(bf16[32,264,384]{2,1,0:T(8,128)(2,1)} %all-to-all-done), kind=kLoop, calls=%fused_computation.123 | loop fusion | bytes 12582912 | tf_op jit(solution)/shard_map/slice | solution.py:113
  209.4 9.0 %reshape.277 = bf16[4096,3,128]{2,1,0:T(4,128)(2,1)} reshape(bf16[32,128,384]{2,1,0:T(8,128)(2,1)} %get-tuple-element.12) | data formatting | bytes 6291456 | tf_op jit(solution)/shard_map/reshape | solution.py:114
  218.4 3.9 %reshape.278 = bf16[4096,3,128]{2,1,0:T(4,128)(2,1)} reshape(bf16[32,128,384]{2,1,0:T(8,128)(2,1)S(1)} %get-tuple-element.11) | data formatting | bytes 6291456 | tf_op jit(solution)/shard_map/reshape | solution.py:113
  222.3 10.1 %bitcast_reduce_fusion = (f32[288,3]{0,1:T(4,128)S(1)}, f32[3,4096,288]{1,2,0:T(8,128)}) fusion(pred[4096]{0:T(1024)(128)(4,1)S(1)} %iota_compare_fusion.1, bf16[4096,3,128]{2,1,0:T(4,128)(2,1)} %reshape.278, bf16[296,3,64]{2,0,1:T(8,128)(2,1)S(1)} %get-tuple-element.13, bf16[296,3,64]{2,0,1:T(8,128)(2,1)} %copy-done.3), kind=kOutput, calls=%fused_computation.3 | convolution fusion | flops 917027968 | bytes 17536384 | tf_op jit(solution)/shard_map/qhd,khd->qhk/dot_general | solution.py:156
  232.4 7.5 %fusion.15 = f32[288,3,128]{2,0,1:T(8,128)S(1)} fusion(bf16[4096,3,128]{2,1,0:T(4,128)(2,1)S(1)} %copy-done.1, f32[3,4096,288]{1,2,0:T(8,128)} %get-tuple-element.33, f32[288,3]{0,1:T(4,128)S(1)} %max.10, pred[4096]{0:T(1024)(128)(4,1)S(1)} %iota_compare_fusion.1), kind=kOutput, calls=%fused_computation.23 | convolution fusion | flops 923664384 | bytes 17751424 | tf_op jit(solution)/shard_map/qhk,khd->qhd/dot_general | solution.py:169
  239.9 9.0 %fusion.2 = f32[288,3]{0,1:T(4,128)S(1)} fusion(f32[3,4096,288]{1,2,0:T(8,128)} %get-tuple-element.33, f32[288,3]{0,1:T(4,128)S(1)} %max.10, pred[4096]{0:T(1024)(128)(4,1)S(1)} %iota_compare_fusion.1), kind=kLoop, calls=%fused_computation.7 | loop fusion | flops 17693856 | bytes 14166784 | tf_op jit(solution)/shard_map/reduce_sum | solution.py:168
  248.9 0.3 fusion.21
  249.2 0.5 fusion.20
  249.8 0.5 broadcast.170
  250.3 2.6 reduce.3
  252.9 1.3 reshape.280
  254.7 0.2 copy.113
  255.0 0.2 copy.110
  255.8 6.4 %fusion.32 = f32[296,5120]{1,0:T(8,128)} fusion(bf16[384,5120]{1,0:T(8,128)(2,1)} %param.22, bf16[8,3,128]{2,0,1:T(8,128)(2,1)S(1)} %divide_convert_fusion, bf16[288,3,128]{2,0,1:T(8,128)(2,1)S(1)} %fusion.20), kind=kOutput, calls=%fused_computation.50 | convolution fusion | flops 1164374016 | bytes 10221568 | tf_op jit(solution)/shard_map/dot_general | solution.py:182
  262.2 57.6 %reduce-scatter.2.cloned.1.call-done = f32[296,640]{1,0:T(8,128)} async-done(((f32[296,5120]{1,0:T(8,128)}), f32[296,640]{1,0:T(8,128)}) %reduce-scatter.2.cloned.1.call-update) | async-done | bytes 757776 | tf_op jit(solution)/shard_map/reduce_scatter | solution.py:183
  319.8 1.3 multiply_reduce_fusion
  321.1 13.1 %psum.23 = f32[296]{0:T(512)S(1)} all-reduce(f32[296]{0:T(512)S(1)} %multiply_reduce_fusion), channel_id=1, replica_groups=mesh['req'=32,'tp'=8] {'tp'}, use_global_device_ids=true, to_apply=%region_17.18 | all-reduce | flops 296 | bytes 2368 | tf_op jit(solution)/shard_map/psum | solution.py:184
  334.2 2.1 add_convert_fusion
  (75 shorter events, 2.6 us)
Async XLA Ops:
  6.5 21.2 %copy-start.10 = (bf16[296,384]{1,0:T(8,128)(2,1)S(1)}, bf16[296,384]{1,0:T(8,128)(2,1)}, u32[]{:S(2)}) copy-start(bf16[296,384]{1,0:T(8,128)(2,1)} %param.18) | copy-start | bytes 681988
  6.5 19.9 %copy-start.17 = (s32[32]{0:T(128)S(1)}, s32[32]{0:T(128)}, u32[]{:S(2)}) copy-start(s32[32]{0:T(128)} %param.31) | copy-start | bytes 388
  6.5 21.2 %copy-start.14 = (f32[384]{0:T(512)S(1)}, f32[384]{0:T(512)}, u32[]{:S(2)}) copy-start(f32[384]{0:T(512)} %param.21) | copy-start | bytes 4612
  8.8 20.7 %copy-start = (s32[256]{0:T(256)S(1)}, s32[256]{0:T(256)}, u32[]{:S(2)}) copy-start(s32[256]{0:T(256)} %param.30) | copy-start | bytes 3076
  29.5 3.7 %copy-start.2 = (bf16[32,1,128,384]{3,2,1,0:T(8,128)(2,1)S(1)}, bf16[32,1,128,384]{3,2,1,0:T(8,128)(2,1)}, u32[]{:S(2)}) copy-start(bf16[32,1,128,384]{3,2,1,0:T(8,128)(2,1)} %param.25) | copy-start | bytes 9437188
  32.3 0.7 copy-start.3
  32.3 0.8 copy-start.6
  32.3 0.8 copy-start.8
  38.3 9.8 %copy-start.11 = (bf16[8,128,384]{2,1,0:T(8,128)(2,1)S(1)}, bf16[8,128,384]{2,1,0:T(8,128)(2,1)}, u32[]{:S(2)}) copy-start(bf16[8,128,384]{2,1,0:T(8,128)(2,1)} %param.26) | copy-start | bytes 2359300
  38.3 10.2 %copy-start.15 = (s32[8]{0:T(128)S(1)}, s32[8]{0:T(128)}, u32[]{:S(2)}) copy-start(s32[8]{0:T(128)} %param.28) | copy-start | bytes 100
  38.3 13.1 %copy-start.18 = (s32[8]{0:T(128)S(1)}, s32[8]{0:T(128)}, u32[]{:S(2)}) copy-start(s32[8]{0:T(128)} %param.29) | copy-start | bytes 100
  38.3 13.9 %copy-start.4 = (bf16[296,3,64]{2,0,1:T(8,128)(2,1)S(1)}, bf16[296,3,64]{2,0,1:T(8,128)(2,1)}, u32[]{:S(2)}) copy-start(bf16[296,3,64]{2,0,1:T(8,128)(2,1)} %copy-done.3) | copy-start | bytes 340996
  38.4 13.9 %copy-start.7 = (bf16[296,3,64]{2,0,1:T(8,128)(2,1)S(1)}, bf16[296,3,64]{2,0,1:T(8,128)(2,1)}, u32[]{:S(2)}) copy-start(bf16[296,3,64]{2,0,1:T(8,128)(2,1)} %copy-done.6) | copy-start | bytes 340996
  38.4 13.9 %copy-start.9 = (bf16[296,3,64]{2,0,1:T(8,128)(2,1)S(1)}, bf16[296,3,64]{2,0,1:T(8,128)(2,1)}, u32[]{:S(2)}) copy-start(bf16[296,3,64]{2,0,1:T(8,128)(2,1)} %copy-done.8) | copy-start | bytes 340996
  38.4 150.0 %all-to-all-start = ((bf16[32,264,384]{2,1,0:T(8,128)(2,1)}), bf16[32,264,384]{2,1,0:T(8,128)(2,1)}, u32[]{:S(2)}, u32[]{:S(2)}) async-start(bf16[32,264,384]{2,1,0:T(8,128)(2,1)} %pad_maximum_fusion), calls=%async_computation | async-start | bytes 12976128 | tf_op jit(solution)/shard_map/all_to_all | solution.py:111
  194.5 55.3 %all-to-all-start.1 = ((f32[32,1,3120]{2,1,0:T(1,128)}), f32[32,1,3120]{2,1,0:T(1,128)}, u32[]{:S(2)}, u32[]{:S(2)}) async-start(f32[32,1,3120]{2,1,0:T(1,128)} %reshape.279), calls=%async_computation.1 | async-start | bytes 819200 | tf_op jit(solution)/shard_map/all_to_all | solution.py:140
  203.7 116.2 %reduce-scatter.2.cloned.1.call-start = ((), (), s32[]{:S(2)}) async-start(), calls=%async_computation.3 | async-start | bytes 6819840 | tf_op jit(solution)/shard_map/reduce_scatter | solution.py:183
  222.3 10.1 %copy-start.1 = (bf16[4096,3,128]{2,1,0:T(4,128)(2,1)S(1)}, bf16[4096,3,128]{2,1,0:T(4,128)(2,1)}, u32[]{:S(2)}) copy-start(bf16[4096,3,128]{2,1,0:T(4,128)(2,1)} %reshape.277) | copy-start | bytes 9437188
  239.9 9.0 %copy-start.5 = (f32[288,3,288]{0,2,1:T(8,128)S(1)}, f32[288,3,288]{0,2,1:T(8,128)}, u32[]{:S(2)}) copy-start(f32[288,3,288]{0,2,1:T(8,128)} %get-tuple-element.35) | copy-start | bytes 2985988
  239.9 9.3 %copy-start.16 = (bf16[296,384]{1,0:T(8,128)(2,1)S(1)}, bf16[296,384]{1,0:T(8,128)(2,1)}, u32[]{:S(2)}) copy-start(bf16[296,384]{1,0:T(8,128)(2,1)} %param.19) | copy-start | bytes 681988
  262.2 72.0 %copy-start.12 = (bf16[296,640]{1,0:T(8,128)(2,1)S(1)}, bf16[296,640]{1,0:T(8,128)(2,1)}, u32[]{:S(2)}) copy-start(bf16[296,640]{1,0:T(8,128)(2,1)} %param.16) | copy-start | bytes 1136644
  262.2 72.0 %copy-start.13 = (f32[640]{0:T(1024)S(1)}, f32[640]{0:T(1024)}, u32[]{:S(2)}) copy-start(f32[640]{0:T(1024)} %param.23) | copy-start | bytes 7684
Sparse Core Ops, SparseCore 0:
  262.4 57.4 reduce-scatter.1

commit v4 on v3

--- a/solution.py
+++ b/solution.py
@@ -101,7 +101,6 @@
     outgoing = jnp.concatenate(
         [
             prefix_keys.reshape(groups, block_rows, local_width),
-            prefix_values.reshape(groups, block_rows, local_width),
             jnp.broadcast_to(
                 query[None, SPAN:].reshape(1, DEC, local_width), (groups, DEC, local_width)
             ),
@@ -109,10 +108,17 @@
         1,
     )
     incoming = lax.all_to_all(outgoing, "req", split_axis=0, concat_axis=0, tiled=True)
+    own_values = lax.all_to_all(
+        prefix_values.reshape(groups, block_rows, local_width),
+        "req",
+        split_axis=0,
+        concat_axis=0,
+        tiled=True,
+    )
     prefix_len = groups * block_rows
     own_keys = incoming[:, :block_rows].reshape(prefix_len, local_heads, HD)
-    own_values = incoming[:, block_rows : 2 * block_rows].reshape(prefix_len, local_heads, HD)
-    decode_queries = incoming[:, 2 * block_rows :].reshape(requests, local_heads, HD)
+    own_values = own_values.reshape(prefix_len, local_heads, HD)
+    decode_queries = incoming[:, block_rows:].reshape(requests, local_heads, HD)
     live_slot = slot_owner >= 0
     owner_index = jnp.maximum(slot_owner, 0)
     slot_queries = decode_queries[owner_index]

time: 345 us -> 316 us (0.916)
  waiting for transfers between devices: 192 us -> 141 us
  local copies, waits for them, and re-layouts: 32.4 us -> 46.7 us
  starting transfers between devices: 19.1 us -> 27.7 us
  matrix products: 27.7 us -> 31.7 us
    all_to_all x1, waiting for transfers between devices: 135 us -> 54.9 us  [body(): lax.all_to_all(outgoing, 'req', split_axis=0, concat_axis=0, tiled=True)]
    all_to_all x0 -> x1, waiting for transfers between devices: none -> 40.5 us  [body(): lax.all_to_all(prefix_values.reshape(groups, block_rows, local_width), 'r...]
    all_to_all x0 -> x1, starting transfers between devices: none -> 12.2 us  [body(): lax.all_to_all(prefix_values.reshape(groups, block_rows, local_width), 'r...]
    reduce_scatter x1, waiting for transfers between devices: 57.6 us -> 45.8 us  [body(): my_share = lax.psum_scatter(partial, 'tp', scatter_dimension=1, tiled=True)]
    unnamed x42 -> x54, local copies, waits for them, and re-layouts: 6.05 us -> 11.5 us
    reshape x1, local copies, waits for them, and re-layouts: 3.91 us -> 9.06 us  [body(): own_keys = incoming[:, :block_rows].reshape(prefix_len, local_heads, HD)]
  transfers between devices with their start and end apart: 3 -> 4, of which waited for: 2 -> 3; matrix products, arithmetic and copies ran while one was open for 15% -> 24% of each run, Pallas kernels for 0% -> 0%
where the time goes in v4:
time: 316 us; the launch traced here: 314 us
  waiting for transfers between devices  141 us (45%)
  local copies, waits for them, and re-layouts  46.7 us (15%)
  matrix products  31.7 us (10%)
  starting transfers between devices  27.7 us (9%)
  other arithmetic  26.9 us (9%)
  blocking collectives  26.1 us (8%)
  between operations  13.8 us (4%)
    all_to_all x1, waiting for transfers between devices, body(): lax.all_to_all(outgoing, 'req', split_axis=0, concat_axis=0, tiled=True)  54.9 us
    reduce_scatter x1, waiting for transfers between devices, body(): my_share = lax.psum_scatter(partial, 'tp', scatter_dimension=1, tiled=True)  45.8 us
    all_to_all x1, waiting for transfers between devices, body(): lax.all_to_all(prefix_values.reshape(groups, block_rows, local_width), 'r...  40.5 us
    psum x1, blocking collectives, body(): power = lax.psum(jnp.sum(my_share * my_share, 1), 'tp')  13.1 us
    psum x1, blocking collectives, body(): lax.psum((jnp.sum(float_query * float_query, 1), jnp.sum(float_key * floa...  13 us
    all_to_all x1, starting transfers between devices, body(): lax.all_to_all(prefix_values.reshape(groups, block_rows, local_width), 'r...  12.2 us
    unnamed x54, local copies, waits for them, and re-layouts  11.5 us
    dot_general x1, matrix products, body(): jnp.einsum('qhd,khd->qhk', span_query, own_keys, preferred_element_type=j...  9.93 us
  transfers between devices with their start and end apart: 4, of which 3 were waited for; matrix products, arithmetic and copies ran while one was open for 24% of the time, Pallas kernels for 0%

profile of v4, /device:TPU:1, one launch (start us, length us, event | category | flops | bytes accessed | tf_op | source)
XLA Modules:
  0.0 314.1 jit_solution(10657967381840136902)
XLA Ops:
  6.5 12.2 %all-to-all-start.1 = ((bf16[32,128,384]{2,1,0:T(8,128)(2,1)}), bf16[32,128,384]{2,1,0:T(8,128)(2,1)S(1)}, u32[]{:S(2)}, u32[]{:S(2)}) async-start(bf16[32,128,384]{2,1,0:T(8,128)(2,1)} %bitcast.88), calls=%async_computation.1 | async-start | bytes 6291456 | tf_op jit(solution)/shard_map/all_to_all | solution.py:111
  18.9 1.1 fusion.24
  20.0 13.0 %all-reduce.1 = (f32[296]{0:T(512)S(1)}, f32[296]{0:T(512)S(1)}) all-reduce(f32[296]{0:T(512)S(1)} %fusion.22, f32[296]{0:T(512)S(1)} %fusion.24), channel_id=1, replica_groups=mesh['req'=32,'tp'=8] {'tp'}, use_global_device_ids=true, to_apply=%region_1.0 | all-reduce | flops 592 | bytes 4736 | tf_op jit(solution)/shard_map/psum | solution.py:83
  33.0 0.9 fusion.23
  33.9 2.0 reshape.243
  35.9 1.8 fusion.25
  37.7 2.0 reshape.245
  39.8 0.6 dynamic_slice.7
  40.5 0.6 iota_add_fusion
  41.2 0.6 multiply_cosine_fusion
  41.8 1.7 fusion.69
  43.5 1.8 fusion.70
  45.6 0.6 copy-done.4
  46.5 2.1 pad_maximum_fusion
  48.5 40.5 %all-to-all-done.1 = bf16[32,128,384]{2,1,0:T(8,128)(2,1)S(1)} async-done(((bf16[32,128,384]{2,1,0:T(8,128)(2,1)}), bf16[32,128,384]{2,1,0:T(8,128)(2,1)S(1)}, u32[]{:S(2)}, u32[]{:S(2)}) %all-to-all-start.1) | async-done | bytes 3145760 | tf_op jit(solution)/shard_map/all_to_all | solution.py:111
  89.0 1.7 copy-done.1
  90.7 7.9 %all-to-all-start = ((bf16[32,136,384]{2,1,0:T(8,128)(2,1)}), bf16[32,136,384]{2,1,0:T(8,128)(2,1)S(1)}, u32[]{:S(2)}, u32[]{:S(2)}) async-start(bf16[32,136,384]{2,1,0:T(8,128)(2,1)} %pad_maximum_fusion), calls=%async_computation | async-start | bytes 6684672 | tf_op jit(solution)/shard_map/all_to_all | solution.py:110
  98.7 2.3 copy.106
  101.0 0.6 gather_fusion
  101.6 2.3 copy.107
  103.9 0.6 iota_compare_fusion.1
  104.8 1.3 bitcast_convert_fusion
  106.1 3.4 %fusion.71 = (f32[288,3]{0,1:T(4,128)}, f32[288,3,288]{0,2,1:T(8,128)}) fusion(bf16[296,3,64]{2,0,1:T(8,128)(2,1)} %copy-done.4, bf16[296,3,64]{2,0,1:T(8,128)(2,1)} %copy-done.6, bf16[296,3,64]{2,0,1:T(8,128)(2,1)} %copy-done.10, bf16[296,3,64]{2,0,1:T(8,128)(2,1)} %copy-done.9, pred[288,288]{0,1:T(8,128)(4,1)S(1)} %iota_compare_fusion), kind=kOutput, calls=%fused_computation.125 | convolution fusion | flops 65331360 | bytes 1536384 | tf_op jit(solution)/shard_map/qhd,khd->qhk/dot_general | solution.py:166
  109.5 9.0 %reshape.278 = bf16[4096,3,128]{2,1,0:T(4,128)(2,1)} reshape(bf16[32,128,384]{2,1,0:T(8,128)(2,1)} %copy-done.1) | data formatting | bytes 6291456 | tf_op jit(solution)/shard_map/reshape | solution.py:120
  118.5 54.9 %all-to-all-done = bf16[32,136,384]{2,1,0:T(8,128)(2,1)S(1)} async-done(((bf16[32,136,384]{2,1,0:T(8,128)(2,1)}), bf16[32,136,384]{2,1,0:T(8,128)(2,1)S(1)}, u32[]{:S(2)}, u32[]{:S(2)}) %all-to-all-start) | async-done | bytes 3342368 | tf_op jit(solution)/shard_map/all_to_all | solution.py:110
  173.4 0.8 reshape.248
  174.2 1.6 gather_fusion.1
  175.9 1.4 fusion.42
  177.9 1.6 fusion.40
  179.5 0.6 convolution_bitcast_fusion
  180.1 0.8 pad_maximum_fusion.1
  180.9 2.3 copy.108
  183.2 3.1 reshape.279
  186.3 7.4 %all-to-all-start.2 = ((f32[32,1,3120]{2,1,0:T(1,128)}), f32[32,1,3120]{2,1,0:T(1,128)}, u32[]{:S(2)}, u32[]{:S(2)}) async-start(f32[32,1,3120]{2,1,0:T(1,128)} %reshape.279), calls=%async_computation.2 | async-start | bytes 819200 | tf_op jit(solution)/shard_map/all_to_all | solution.py:146
  193.9 2.2 slice.74
  196.1 9.1 %reshape.277 = bf16[4096,3,128]{2,1,0:T(4,128)(2,1)} reshape(bf16[32,128,384]{2,1,0:T(8,128)(2,1)} %slice.74) | data formatting | bytes 6291456 | tf_op jit(solution)/shard_map/reshape | solution.py:119
  205.2 9.9 %bitcast_reduce_fusion = (f32[288,3]{0,1:T(4,128)S(1)}, f32[3,4096,288]{1,2,0:T(8,128)}) fusion(pred[4096]{0:T(1024)(128)(4,1)S(1)} %iota_compare_fusion.1, bf16[4096,3,128]{2,1,0:T(4,128)(2,1)} %reshape.277, bf16[296,3,64]{2,0,1:T(8,128)(2,1)S(1)} %copy-done.5, bf16[296,3,64]{2,0,1:T(8,128)(2,1)S(1)} %copy-done.7), kind=kOutput, calls=%fused_computation.3 | convolution fusion | flops 917027968 | bytes 17536384 | tf_op jit(solution)/shard_map/qhd,khd->qhk/dot_general | solution.py:162
  215.1 7.5 %fusion.4 = f32[3,288,128]{2,1,0:T(8,128)S(1)} fusion(f32[3,4096,288]{1,2,0:T(8,128)} %get-tuple-element.31, f32[288,3]{0,1:T(4,128)S(1)} %max.10, pred[4096]{0:T(1024)(128)(4,1)S(1)} %iota_compare_fusion.1, bf16[4096,3,128]{2,1,0:T(4,128)(2,1)S(1)} %copy-done.2), kind=kOutput, calls=%fused_computation.9 | convolution fusion | flops 923664384 | bytes 17751424 | tf_op jit(solution)/shard_map/qhk,khd->qhd/dot_general | solution.py:175
  222.7 9.0 %fusion.2 = f32[288,3]{0,1:T(4,128)S(1)} fusion(f32[3,4096,288]{1,2,0:T(8,128)} %get-tuple-element.31, f32[288,3]{0,1:T(4,128)S(1)} %max.10, pred[4096]{0:T(1024)(128)(4,1)S(1)} %iota_compare_fusion.1), kind=kLoop, calls=%fused_computation.7 | loop fusion | flops 17693856 | bytes 14166784 | tf_op jit(solution)/shard_map/reduce_sum | solution.py:174
  232.0 0.5 fusion.15
  232.6 0.5 broadcast.170
  233.1 2.6 reduce.3
  235.7 1.3 reshape.280
  238.6 6.4 %fusion.27 = f32[296,5120]{1,0:T(8,128)} fusion(bf16[384,5120]{1,0:T(8,128)(2,1)} %param.22, bf16[8,3,128]{2,0,1:T(8,128)(2,1)S(1)} %divide_convert_fusion, bf16[288,3,128]{2,0,1:T(8,128)(2,1)S(1)} %fusion.15), kind=kOutput, calls=%fused_computation.49 | convolution fusion | flops 1164374016 | bytes 10221568 | tf_op jit(solution)/shard_map/dot_general | solution.py:188
  245.0 45.8 %reduce-scatter.2.cloned.1.call-done = f32[296,640]{1,0:T(8,128)} async-done(((f32[296,5120]{1,0:T(8,128)}), f32[296,640]{1,0:T(8,128)}) %reduce-scatter.2.cloned.1.call-update) | async-done | bytes 757776 | tf_op jit(solution)/shard_map/reduce_scatter | solution.py:189
  290.8 1.3 multiply_reduce_fusion
  292.1 13.1 %psum.23 = f32[296]{0:T(512)S(1)} all-reduce(f32[296]{0:T(512)S(1)} %multiply_reduce_fusion), channel_id=1, replica_groups=mesh['req'=32,'tp'=8] {'tp'}, use_global_device_ids=true, to_apply=%region_17.18 | all-reduce | flops 296 | bytes 2368 | tf_op jit(solution)/shard_map/psum | solution.py:190
  305.2 2.1 add_convert_fusion
  (89 shorter events, 3.7 us)
Async XLA Ops:
  6.5 12.2 %copy-start.11 = (bf16[296,384]{1,0:T(8,128)(2,1)S(1)}, bf16[296,384]{1,0:T(8,128)(2,1)}, u32[]{:S(2)}) copy-start(bf16[296,384]{1,0:T(8,128)(2,1)} %param.17) | copy-start | bytes 681988
  6.5 26.5 %copy-start.19 = (f32[384]{0:T(512)S(1)}, f32[384]{0:T(512)}, u32[]{:S(2)}) copy-start(f32[384]{0:T(512)} %param.20) | copy-start | bytes 4612
  6.5 29.4 %copy-start.20 = (f32[384]{0:T(512)S(1)}, f32[384]{0:T(512)}, u32[]{:S(2)}) copy-start(f32[384]{0:T(512)} %param.21) | copy-start | bytes 4612
  6.5 33.2 %copy-start = (s32[256]{0:T(256)S(1)}, s32[256]{0:T(256)}, u32[]{:S(2)}) copy-start(s32[256]{0:T(256)} %param.30) | copy-start | bytes 3076
  6.5 33.3 %copy-start.23 = (s32[32]{0:T(128)S(1)}, s32[32]{0:T(128)}, u32[]{:S(2)}) copy-start(s32[32]{0:T(128)} %param.31) | copy-start | bytes 388
  6.5 82.5 %all-to-all-start.1 = ((bf16[32,128,384]{2,1,0:T(8,128)(2,1)}), bf16[32,128,384]{2,1,0:T(8,128)(2,1)S(1)}, u32[]{:S(2)}, u32[]{:S(2)}) async-start(bf16[32,128,384]{2,1,0:T(8,128)(2,1)} %bitcast.88), calls=%async_computation.1 | async-start | bytes 6291456 | tf_op jit(solution)/shard_map/all_to_all | solution.py:111
  43.5 3.0 copy-start.3
  45.5 0.7 copy-start.4
  45.5 0.8 copy-start.6
  45.5 0.8 copy-start.9
  45.6 0.9 copy-start.10
  48.5 52.4 %copy-start.21 = (s32[8]{0:T(128)S(1)}, s32[8]{0:T(128)}, u32[]{:S(2)}) copy-start(s32[8]{0:T(128)} %param.28) | copy-start | bytes 100
  48.5 56.1 %copy-start.24 = (s32[8]{0:T(128)S(1)}, s32[8]{0:T(128)}, u32[]{:S(2)}) copy-start(s32[8]{0:T(128)} %param.29) | copy-start | bytes 100
  89.0 1.7 copy-start.1
  90.7 82.7 %all-to-all-start = ((bf16[32,136,384]{2,1,0:T(8,128)(2,1)}), bf16[32,136,384]{2,1,0:T(8,128)(2,1)S(1)}, u32[]{:S(2)}, u32[]{:S(2)}) async-start(bf16[32,136,384]{2,1,0:T(8,128)(2,1)} %pad_maximum_fusion), calls=%async_computation | async-start | bytes 6684672 | tf_op jit(solution)/shard_map/all_to_all | solution.py:110
  101.0 17.5 %copy-start.16 = (s32[1024]{0:T(1024)}, s32[1024]{0:T(1024)S(1)}, u32[]{:S(2)}) copy-start(s32[1024]{0:T(1024)S(1)} %pad_clamp_fusion) | copy-start | bytes 12292
  104.6 1.5 copy-start.12
  186.3 46.3 %all-to-all-start.2 = ((f32[32,1,3120]{2,1,0:T(1,128)}), f32[32,1,3120]{2,1,0:T(1,128)}, u32[]{:S(2)}, u32[]{:S(2)}) async-start(f32[32,1,3120]{2,1,0:T(1,128)} %reshape.279), calls=%async_computation.2 | async-start | bytes 819200 | tf_op jit(solution)/shard_map/all_to_all | solution.py:146
  193.7 97.2 %reduce-scatter.2.cloned.1.call-start = ((), (), s32[]{:S(2)}) async-start(), calls=%async_computation.4 | async-start | bytes 6819840 | tf_op jit(solution)/shard_map/reduce_scatter | solution.py:189
  196.1 9.1 %copy-start.5 = (bf16[296,3,64]{2,0,1:T(8,128)(2,1)S(1)}, bf16[296,3,64]{2,0,1:T(8,128)(2,1)}, u32[]{:S(2)}) copy-start(bf16[296,3,64]{2,0,1:T(8,128)(2,1)} %copy-done.4) | copy-start | bytes 340996
  196.1 9.1 %copy-start.7 = (bf16[296,3,64]{2,0,1:T(8,128)(2,1)S(1)}, bf16[296,3,64]{2,0,1:T(8,128)(2,1)}, u32[]{:S(2)}) copy-start(bf16[296,3,64]{2,0,1:T(8,128)(2,1)} %copy-done.6) | copy-start | bytes 340996
  205.2 9.9 %copy-start.17 = (f32[288,3]{0,1:T(4,128)S(1)}, f32[288,3]{0,1:T(4,128)}, u32[]{:S(2)}) copy-start(f32[288,3]{0,1:T(4,128)} %get-tuple-element.32) | copy-start | bytes 10372
  205.2 9.9 %copy-start.2 = (bf16[4096,3,128]{2,1,0:T(4,128)(2,1)S(1)}, bf16[4096,3,128]{2,1,0:T(4,128)(2,1)}, u32[]{:S(2)}) copy-start(bf16[4096,3,128]{2,1,0:T(4,128)(2,1)} %reshape.278) | copy-start | bytes 9437188
  222.7 9.0 %copy-start.8 = (f32[288,3,288]{0,2,1:T(8,128)S(1)}, f32[288,3,288]{0,2,1:T(8,128)}, u32[]{:S(2)}) copy-start(f32[288,3,288]{0,2,1:T(8,128)} %get-tuple-element.33) | copy-start | bytes 2985988
  222.7 9.0 %copy-start.13 = (pred[288,288]{0,1:T(8,128)(4,1)S(1)}, pred[288,288]{0,1:T(8,128)(4,1)}, u32[]{:S(2)}) copy-start(pred[288,288]{0,1:T(8,128)(4,1)} %copy-done.12) | copy-start | bytes 248836
  222.7 9.3 %copy-start.22 = (bf16[296,384]{1,0:T(8,128)(2,1)S(1)}, bf16[296,384]{1,0:T(8,128)(2,1)}, u32[]{:S(2)}) copy-start(bf16[296,384]{1,0:T(8,128)(2,1)} %param.19) | copy-start | bytes 681988
  232.5 5.8 %copy-start.15 = (f32[1,8,3,128]{3,1,0,2:T(8,128)S(1)}, f32[1,8,3,128]{3,1,0,2:T(8,128)}, u32[]{:S(2)}) copy-start(f32[1,8,3,128]{3,1,0,2:T(8,128)} %bitcast_convert_fusion) | copy-start | bytes 36868
  245.0 60.2 %copy-start.14 = (bf16[296,640]{1,0:T(8,128)(2,1)S(1)}, bf16[296,640]{1,0:T(8,128)(2,1)}, u32[]{:S(2)}) copy-start(bf16[296,640]{1,0:T(8,128)(2,1)} %param.16) | copy-start | bytes 1136644
  245.0 60.2 %copy-start.18 = (f32[640]{0:T(1024)S(1)}, f32[640]{0:T(1024)}, u32[]{:S(2)}) copy-start(f32[640]{0:T(1024)} %param.23) | copy-start | bytes 7684
Sparse Core Ops, SparseCore 0:
  245.2 45.6 reduce-scatter.1
